TPU v7x, 32 devices: a whole 2x2x4 slice. The times are simulated.
32 devices in a mesh: gz: 2 (over core), gx: 4 (over y, x), gy: 4 (over z).
Axes of the slice: x: 2, y: 2, z: 4, core: 2. Of those that a mesh axis runs over, the one named last changes fastest.
Arguments:
- positions: float32 [128, 3, 16384], P(('gz', 'gy'), None, 'gx'), may hold values from -8 to 8
- diffusion_noise: float32 [128, 3, 16384], P(('gz', 'gy'), None, 'gx'), may hold values from -5 to 5
- base_nuclei: float32 [16, 3], replicated, may hold values from -4.15 to 4.15, as said below
- displacements: float32 [8, 16, 3], replicated, may hold values from -0.4375 to 0.4375
- charges: float32 [16], replicated, may hold values from 2 to 14
- orbital_decay: float32 [16], replicated, may hold values from 0.6 to 2
- coefficients: float32 [16], replicated, may hold values from 0.5 to 2
- weights: float32 [16384], P('gx'), may hold values from 0.5 to 2
- counts: int32 [128], P('gx'), may hold values from 1 to 128
- branch_source: int32 [128], replicated, may hold values from 0 to 127, as said below
Outputs:
- local_energy: float32 [8, 16384], P('gz', 'gx')
- energy_estimate: float32 [8], P('gz')
- new_positions: float32 [128, 3, 16384], P(('gz', 'gy'), None, 'gx')
- new_weights: float32 [16384], P('gx')
Inputs may be any that keep to these rules, and one draw needn't show every extreme that they name: `branch_source`: A permutation of the blocks. Of the 32 destination blocks of each aligned group (d // 32 equal), at most 16 have sources in any one aligned group of 32 source blocks, and some pair reaches 16 for every group, as sender and as receiver. `base_nuclei`: any two nuclei lie 1.7 or more apart.
All inputs are finite; a program needn't handle non-finite values.
Results may differ from a plain program's by a relative error of at most 0.0002.
Values sent between devices are 32-bit elements; how exact they have to be, the bound alone decides.
A program may use at most 128 MiB of HBM per device.

v0:
```python
import functools
import math

import jax
import jax.numpy as jnp
from jax import lax
from jax.experimental import pallas as pl
from jax.experimental.pallas import tpu as pltpu
from jax.sharding import PartitionSpec as P

BLK = 128
NA = 16
SOFT = 0.04
TIME_STEP = 0.01
STEP_ROOT = 0.1
ROWS = 16
LOG2E = 1.4426950408889634


def orbital_rows(consts, g, rows):
    x, y, z = rows
    square = x * x + y * y + z * z
    zero = jnp.zeros_like(x)
    phi = gx = gy = gz = s_w = s_z = s_p = pot = zero
    for a in range(NA):

        def const(n):
            return consts[g, a, n : n + 1, :]

        cx, cy, cz = const(0), const(1), const(2)
        q = square + (const(3) - (x * const(8) + y * const(9) + z * const(10)))
        ri = lax.rsqrt(q)
        e = jnp.exp2(const(4) - const(5) * (q * ri))
        ze = const(6) * e
        w = ze * ri
        z2e = const(6) * ze
        phi = phi + e
        s_w = s_w + w
        gx = gx + w * cx
        gy = gy + w * cy
        gz = gz + w * cz
        s_z = s_z + z2e
        s_p = s_p + (z2e + w) * (ri * ri)
        pot = pot + const(7) * ri
    inverse = 1.0 / phi
    lap = (s_z - 2.0 * s_w - SOFT * s_p) * inverse
    grad = ((gx - x * s_w) * inverse, (gy - y * s_w) * inverse, (gz - z * s_w) * inverse)
    return jnp.log(phi), grad, lap, pot


def geometry_kernel(first, count, own, sources, consts, pos, jgrad, energy, logs):
    electrons = own * sources
    lanes = pos.shape[-1]

    def geometry(step, carry):
        g = first + step

        def slab(n, running):
            rows = [jgrad[0, 3 + c, pl.ds(n * ROWS, ROWS), :] for c in range(3)]
            jrow = [jgrad[0, c, pl.ds(n * ROWS, ROWS), :] for c in range(3)]
            log_phi, grad, lap, pot = orbital_rows(consts, g, rows)
            dot = grad[0] * jrow[0] + grad[1] * jrow[1] + grad[2] * jrow[2]
            return (running[0] + (pot - 0.5 * lap - dot), running[1] + log_phi)

        zero = jnp.zeros((ROWS, lanes), jnp.float32)
        e, l = lax.fori_loop(0, electrons // ROWS, slab, (zero, zero))
        energy[0, pl.ds(step, 1), :] = jnp.sum(e, axis=0, keepdims=True)
        logs[0, pl.ds(step, 1), :] = jnp.sum(l, axis=0, keepdims=True)
        return carry

    lax.fori_loop(0, count, geometry, 0)


def pair_kernel(own, sources, consts, pos, drift, jgrad, energy, base, twice, shifted, counter, direct):
    electrons = own * sources
    lanes = pos.shape[-1]
    groups = electrons // 8
    half = groups // 2
    for c in range(3):
        for s in range(sources):
            block = pos[s, 0, c]
            jgrad[0, 3 + c, s * own : (s + 1) * own, :] = block
            twice[c, s * own : (s + 1) * own, :] = block
        twice[c, electrons : electrons + 8, :] = twice[c, 0:8, :]
        for k in range(8):
            shifted[k, c] = twice[c, k : k + electrons, :]
    counter[...] = jnp.zeros_like(counter)
    direct[...] = jnp.zeros_like(direct)

    def interact(k, i, steps, total):
        mine = [shifted[0, c, pl.ds(pl.multiple_of(i * 8, 8), 8), :] for c in range(3)]
        acc = [direct[c, pl.ds(pl.multiple_of(i * 8, 8), 8), :] for c in range(3)]
        for m in steps:
            j = lax.rem(i + m, groups)
            at = pl.ds(pl.multiple_of(j * 8, 8), 8)
            v = [mine[c] - shifted[k, c, at, :] for c in range(3)]
            q = (v[0] * v[0] + v[1] * v[1]) + (v[2] * v[2] + SOFT)
            ri = lax.rsqrt(q)
            root = lax.rsqrt(1.0 + q * ri)
            t = root * root
            t2 = t * t
            a = t2 * ri
            total = total + (ri + (t2 * t - a) - (SOFT * (ri * ri)) * (t2 * t + 0.5 * a))
            for c in range(3):
                f = a * v[c]
                acc[c] = acc[c] + f
                counter[k, c, at, :] = counter[k, c, at, :] + f
        for c in range(3):
            direct[c, pl.ds(pl.multiple_of(i * 8, 8), 8), :] = acc[c]
        return total

    total = jnp.zeros((8, lanes), jnp.float32)
    total = lax.fori_loop(0, groups, lambda i, e: interact(0, i, range(1, half), e), total)
    total = lax.fori_loop(0, half, lambda i, e: interact(0, i, (half,), e), total)

    def shifted_groups(n, e):
        return interact(1 + n // groups, lax.rem(n, groups), range(half), e)

    total = lax.fori_loop(0, 7 * groups, shifted_groups, total)
    square = jnp.zeros((electrons, lanes), jnp.float32)
    for c in range(3):
        back = counter[0, c]
        for k in range(1, 8):
            back = back + pltpu.roll(counter[k, c], k, 0)
        value = 0.5 * (direct[c] - back)
        jgrad[0, c] = value
        square = square + value * value
    base[0] = jnp.broadcast_to(
        jnp.sum(total, axis=0, keepdims=True) - 0.5 * jnp.sum(square, axis=0, keepdims=True),
        (8, lanes),
    )
    e_sum = jnp.zeros((1, lanes), jnp.float32)

    def slab(n, e_sum):
        at = pl.ds(pl.multiple_of(n * own, own), own)
        rows = [jgrad[0, 3 + c, at, :] for c in range(3)]
        jrow = [jgrad[0, c, at, :] for c in range(3)]
        log_phi, grad, lap, pot = orbital_rows(consts, 0, rows)
        dot = grad[0] * jrow[0] + grad[1] * jrow[1] + grad[2] * jrow[2]
        for c in range(3):
            drift[n, 0, c] = TIME_STEP * (grad[c] + jrow[c])
        return (e_sum[0] + (pot - 0.5 * lap - dot), e_sum[1] + log_phi)

    zero = jnp.zeros((own, lanes), jnp.float32)
    e, l = lax.fori_loop(0, sources, slab, (zero, zero))
    energy[0, 0:1, :] = jnp.sum(e, axis=0, keepdims=True)
    energy[0, 1:2, :] = jnp.sum(l, axis=0, keepdims=True)


def pack_kernel(blocks_here, capacity, source_ref, me_ref, pos, drift, noise, sent, count):
    me = me_ref[0]
    peers = count.shape[0]
    for p in range(peers):
        count[p] = 0

    def one(d, carry):
        source = source_ref[d]
        block = source - me * blocks_here

        @pl.when((block >= 0) & (block < blocks_here))
        def _():
            peer = d // blocks_here
            slot = count[peer]
            count[peer] = slot + 1
            sent[peer * capacity + slot] = pos[block] + drift[block] + STEP_ROOT * noise[block]

        return carry

    lax.fori_loop(0, source_ref.shape[0], one, 0)


def unpack_kernel(blocks_here, capacity, source_ref, me_ref, received, out, count):
    me = me_ref[0]
    peers = count.shape[0]
    for p in range(peers):
        count[p] = 0

    def one(d, carry):
        peer = source_ref[me * blocks_here + d] // blocks_here
        slot = count[peer]
        count[peer] = slot + 1
        out[d] = received[peer * capacity + slot]
        return carry

    lax.fori_loop(0, blocks_here, one, 0)


def nuclear_repulsion(centers, charges):
    offsets = centers[:, :, None, :] - centers[:, None, :, :]
    identity = jnp.eye(centers.shape[1], dtype=jnp.float32)
    distance = jnp.sqrt(jnp.sum(offsets * offsets, axis=3) + identity)
    products = charges[:, None] * charges[None, :] * (1.0 - identity)
    return 0.5 * jnp.sum(products / distance, axis=(1, 2))


def local(
    positions,
    diffusion_noise,
    base_nuclei,
    displacements,
    charges,
    orbital_decay,
    coefficients,
    weights,
    counts,
    branch_source,
):
    own, _, walkers = positions.shape
    geometries = displacements.shape[0]
    sources = lax.axis_size(("gz", "gy"))
    peers = lax.axis_size("gx")
    electrons = own * sources
    per_replica = geometries // lax.axis_size("gz")
    blocks_here = counts.shape[0]
    mine = blocks_here // sources
    local_walkers = walkers // sources
    replica = lax.axis_index(("gz", "gy"))
    device = lax.axis_index("gx")

    def to_blocks(x):
        return x.reshape(own, 3, blocks_here, BLK).transpose(2, 1, 0, 3)

    pos_blocks = to_blocks(positions)
    noise_blocks = to_blocks(diffusion_noise)
    arrived = lax.all_to_all(pos_blocks, ("gz", "gy"), split_axis=0, concat_axis=0, tiled=True)
    arrived = arrived.reshape(sources, mine, 3, own, BLK)

    centers = base_nuclei[None, :, :] + displacements
    shape = (geometries, NA)
    per_nucleus = [
        centers[:, :, 0],
        centers[:, :, 1],
        centers[:, :, 2],
        jnp.sum(centers * centers, axis=2) + SOFT,
        jnp.broadcast_to(jnp.log2(coefficients), shape),
        jnp.broadcast_to(orbital_decay * LOG2E, shape),
        jnp.broadcast_to(orbital_decay, shape),
        jnp.broadcast_to(-charges, shape),
        2.0 * centers[:, :, 0],
        2.0 * centers[:, :, 1],
        2.0 * centers[:, :, 2],
    ]
    table = jnp.stack(per_nucleus + [jnp.zeros(shape, jnp.float32)] * 5, axis=2)
    table = jnp.broadcast_to(table[..., None], table.shape + (BLK,))

    lane_spec = pl.BlockSpec((1, 8, BLK), lambda b: (b, 0, 0))
    table_spec = pl.BlockSpec(table.shape, lambda b: (0, 0, 0, 0))
    pos_spec = pl.BlockSpec((sources, 1, 3, own, BLK), lambda b: (0, b, 0, 0, 0))
    grad_spec = pl.BlockSpec((1, 6, electrons, BLK), lambda b: (b, 0, 0, 0))
    lane_shape = jax.ShapeDtypeStruct((mine, 8, BLK), jnp.float32)
    grad_shape = jax.ShapeDtypeStruct((mine, 6, electrons, BLK), jnp.float32)
    drift, jgrad, first, base = pl.pallas_call(
        functools.partial(pair_kernel, own, sources),
        grid=(mine,),
        in_specs=[table_spec, pos_spec],
        out_specs=[pos_spec, grad_spec, lane_spec, lane_spec],
        out_shape=[
            jax.ShapeDtypeStruct(arrived.shape, jnp.float32),
            grad_shape,
            lane_shape,
            lane_shape,
        ],
        scratch_shapes=[
            pltpu.VMEM((3, electrons + 8, BLK), jnp.float32),
            pltpu.VMEM((8, 3, electrons, BLK), jnp.float32),
            pltpu.VMEM((8, 3, electrons, BLK), jnp.float32),
            pltpu.VMEM((3, electrons, BLK), jnp.float32),
        ],
        compiler_params=pltpu.CompilerParams(vmem_limit_bytes=32 * 2**20),
        cost_estimate=pl.CostEstimate(flops=100_000_000, bytes_accessed=4_000_000, transcendentals=0),
        name="pairs",
    )(table, arrived)

    def more(start, count):
        return pl.pallas_call(
            functools.partial(geometry_kernel, start, count, own, sources),
            grid=(mine,),
            in_specs=[table_spec, pos_spec, grad_spec],
            out_specs=[lane_spec, lane_spec],
            out_shape=[lane_shape, lane_shape],
            compiler_params=pltpu.CompilerParams(vmem_limit_bytes=16 * 2**20),
            cost_estimate=pl.CostEstimate(
                flops=count * 30_000_000, bytes_accessed=8_000_000, transcendentals=0
            ),
            name=f"geometries_{start}",
        )(table, arrived, jgrad)

    split = max(1, (geometries - 1) // 2)
    energy_a, log_a = more(1, split)
    energy_b, log_b = more(1 + split, geometries - 1 - split)

    drift_back = lax.all_to_all(
        drift.reshape(blocks_here, 3, own, BLK), ("gz", "gy"), split_axis=0, concat_axis=0, tiled=True
    )
    capacity = min(blocks_here, max(2, 2 * blocks_here // peers))
    me = device.astype(jnp.int32).reshape(1)
    smem = pl.BlockSpec(memory_space=pltpu.SMEM)
    vmem = pl.BlockSpec(memory_space=pltpu.VMEM)
    sent = pl.pallas_call(
        functools.partial(pack_kernel, blocks_here, capacity),
        in_specs=[smem, smem, vmem, vmem, vmem],
        out_specs=vmem,
        out_shape=jax.ShapeDtypeStruct((peers * capacity, 3, own, BLK), jnp.float32),
        scratch_shapes=[pltpu.SMEM((peers,), jnp.int32)],
        name="pack",
    )(branch_source, me, pos_blocks, drift_back, noise_blocks)
    received = lax.all_to_all(sent, "gx", split_axis=0, concat_axis=0, tiled=True)
    new_blocks = pl.pallas_call(
        functools.partial(unpack_kernel, blocks_here, capacity),
        in_specs=[smem, smem, vmem],
        out_specs=vmem,
        out_shape=jax.ShapeDtypeStruct((blocks_here, 3, own, BLK), jnp.float32),
        scratch_shapes=[pltpu.SMEM((peers,), jnp.int32)],
        name="unpack",
    )(branch_source, me, received)
    new_positions = new_blocks.transpose(2, 1, 0, 3).reshape(own, 3, walkers)

    energies = jnp.concatenate(
        [first[:, 0:1], energy_a[:, :split], energy_b[:, : geometries - 1 - split]], axis=1
    )
    log_sums = jnp.concatenate(
        [first[:, 1:2], log_a[:, :split], log_b[:, : geometries - 1 - split]], axis=1
    )
    nuclear = nuclear_repulsion(centers, charges)
    energies = (energies + base[:, 0:1] + nuclear[None, :, None]) * (1.0 / electrons)
    my_weights = lax.dynamic_slice_in_dim(weights.reshape(blocks_here, BLK), replica * mine, mine, 0)
    my_counts = lax.dynamic_slice_in_dim(counts, replica * mine, mine, 0)
    alive_weights = my_weights * (
        jnp.arange(BLK, dtype=jnp.int32)[None, :] < my_counts[:, None]
    ).astype(jnp.float32)
    omega = alive_weights[:, None, :] * jnp.exp(2.0 * (log_sums - log_sums[:, 0:1]))
    sums = jnp.concatenate([jnp.sum(omega * energies, axis=(0, 2)), jnp.sum(omega, axis=(0, 2))])
    sums = jnp.pad(sums, (0, local_walkers - 2 * geometries)).reshape(mine, 1, BLK)
    bundle = jnp.concatenate([energies, alive_weights[:, None, :], sums], axis=1)
    gathered = lax.all_gather(bundle, ("gx", "gz", "gy"), axis=0, tiled=False)
    total = jnp.sum(
        gathered[:, :, geometries + 1, :].reshape(-1, local_walkers)[:, : 2 * geometries], axis=0
    )
    estimate = total[:geometries] / total[geometries:]
    first_geometry = lax.axis_index("gz") * per_replica
    rows = gathered.reshape(peers, sources * mine, geometries + 2, BLK)
    ours = lax.dynamic_slice(
        rows, (device, 0, first_geometry, 0), (1, sources * mine, per_replica, BLK)
    )
    local_energy = ours[0].transpose(1, 0, 2).reshape(per_replica, walkers)
    kept = rows[:, :, geometries, :] * jnp.exp(estimate[0] - rows[:, :, 0, :])
    kept = kept.reshape(peers * blocks_here, BLK)
    my_sources = lax.dynamic_slice_in_dim(branch_source, device * blocks_here, blocks_here, 0)
    new_weights = jnp.take(kept, my_sources, axis=0).reshape(walkers)
    my_estimate = lax.dynamic_slice_in_dim(estimate, first_geometry, per_replica, 0)
    return (local_energy, my_estimate, new_positions, new_weights)


def solution(mesh):
    in_specs = (
        P(("gz", "gy"), None, "gx"),
        P(("gz", "gy"), None, "gx"),
        P(),
        P(),
        P(),
        P(),
        P(),
        P("gx"),
        P("gx"),
        P(),
    )
    out_specs = (P("gz", "gx"), P("gz"), P(("gz", "gy"), None, "gx"), P("gx"))
    return jax.shard_map(local, mesh=mesh, in_specs=in_specs, out_specs=out_specs, check_vma=False)
```

profile of v0, /device:TPU:0, one launch (start us, length us, event | category | flops | bytes accessed | tf_op | source)
XLA Modules:
  0.0 213.1 jit_solution(18067268771698600392)
XLA Ops:
  0.7 1.1 copy-done
  1.8 0.9 bitcast_bitcast_fusion.1.pos
  2.7 6.5 %all-to-all-start = ((f32[32,3,16,128]{3,2,1,0:T(8,128)}), f32[32,3,16,128]{3,2,1,0:T(8,128)S(1)}, u32[]{:S(2)}, u32[]{:S(2)}) async-start(f32[32,3,16,128]{3,2,1,0:T(8,128)} %bitcast_bitcast_fusion.1.pos), calls=%async_computation | async-start | bytes 1572864 | tf_op jit(solution)/shard_map/all_to_all | solution.py:225
  9.2 0.1 copy.53
  9.4 0.1 copy.54
  9.5 0.1 copy.55
  9.6 0.1 copy.56
  10.3 0.2 stack.12
  10.9 0.2 multiply_reduce_fusion.1
  11.0 18.5 %all-to-all-done = f32[32,3,16,128]{3,2,1,0:T(8,128)S(1)} async-done(((f32[32,3,16,128]{3,2,1,0:T(8,128)}), f32[32,3,16,128]{3,2,1,0:T(8,128)S(1)}, u32[]{:S(2)}, u32[]{:S(2)}) %all-to-all-start) | async-done | bytes 786464 | tf_op jit(solution)/shard_map/all_to_all | solution.py:225
  29.6 0.3 broadcast_in_dim.13.consts
  29.9 45.0 %pairs.1 = (f32[8,4,3,16,128]{4,3,2,1,0:T(8,128)}, f32[4,6,128,128]{3,2,1,0:T(8,128)S(1)}, f32[4,8,128]{2,1,0:T(8,128)S(1)}, f32[4,8,128]{2,1,0:T(8,128)S(1)}) custom-call(f32[8,16,16,128]{3,2,1,0:T(8,128)S(1)} %broadcast_in_dim.13.consts, f32[8,4,3,16,128]{4,3,2,1,0:T(8,128)S(1)} %bitcast.49), custom_call_target="tpu_custom_call" | custom-call | flops 100000000 | bytes 4000000 | tf_op jit(solution)/shard_map/pairs/pallas_call | solution.py:252
  74.9 1.2 copy-done.1
  76.1 3.5 %all-to-all-start.1 = ((f32[32,3,16,128]{3,2,1,0:T(8,128)}), f32[32,3,16,128]{3,2,1,0:T(8,128)S(1)}, u32[]{:S(2)}, u32[]{:S(2)}) async-start(f32[32,3,16,128]{3,2,1,0:T(8,128)} %bitcast.13), calls=%async_computation.1 | async-start | bytes 1572864 | tf_op jit(solution)/shard_map/all_to_all | solution.py:292
  79.7 0.9 dynamic-slice_select_fusion
  80.5 2.1 bitcast_bitcast_fusion.noise
  82.6 18.9 %geometries_4.1 = (f32[4,8,128]{2,1,0:T(8,128)S(1)}, f32[4,8,128]{2,1,0:T(8,128)S(1)}) custom-call(f32[8,16,16,128]{3,2,1,0:T(8,128)S(1)} %broadcast_in_dim.13.consts, f32[8,4,3,16,128]{4,3,2,1,0:T(8,128)S(1)} %bitcast.50, f32[4,6,128,128]{3,2,1,0:T(8,128)S(1)} %copy-done.2), custom_call_target="tpu_custom_call" | custom-call | flops 120000000 | bytes 8000000 | tf_op jit(solution)/shard_map/geometries_4/pallas_call | solution.py:275
  101.5 14.2 %geometries_1.1 = (f32[4,8,128]{2,1,0:T(8,128)S(1)}, f32[4,8,128]{2,1,0:T(8,128)S(1)}) custom-call(f32[8,16,16,128]{3,2,1,0:T(8,128)S(1)} %broadcast_in_dim.13.consts, f32[8,4,3,16,128]{4,3,2,1,0:T(8,128)S(1)} %bitcast.51, f32[4,6,128,128]{3,2,1,0:T(8,128)S(1)} %copy-done.2), custom_call_target="tpu_custom_call" | custom-call | flops 90000000 | bytes 8000000 | tf_op jit(solution)/shard_map/geometries_1/pallas_call | solution.py:275
  115.8 0.2 multiply_reduce_fusion.2
  116.1 0.9 copy-done.4
  117.0 5.0 %pack.1 = f32[64,3,16,128]{3,2,1,0:T(8,128)} custom-call(s32[128]{0:T(128)} %source_ref.3, s32[1]{0:T(128)} %bitcast.12.me_ref, f32[32,3,16,128]{3,2,1,0:T(8,128)} %bitcast_bitcast_fusion.1.pos, f32[32,3,16,128]{3,2,1,0:T(8,128)} %copy-done.4, f32[32,3,16,128]{3,2,1,0:T(8,128)} %bitcast_bitcast_fusion.noise), custom_call_target="tpu_custom_call" | custom-call | tf_op jit(solution)/shard_map/pack/pallas_call | solution.py:299
  122.0 3.7 %all-to-all-start.2 = ((f32[64,3,16,128]{3,2,1,0:T(8,128)}), f32[64,3,16,128]{3,2,1,0:T(8,128)S(1)}, u32[]{:S(2)}, u32[]{:S(2)}) async-start(f32[64,3,16,128]{3,2,1,0:T(8,128)} %pack.1), calls=%async_computation.2 | async-start | bytes 3145728 | tf_op jit(solution)/shard_map/all_to_all | solution.py:307
  125.8 78.1 %all-gather = f32[128,10,128]{2,1,0:T(8,128)S(1)} all-gather(f32[4,10,128]{2,1,0:T(8,128)S(1)} %pad_maximum_fusion), channel_id=2, replica_groups=mesh['gz'=2,'gx'=4,'gy'=4] {'gx','gz','gy'}, dimensions={0}, use_global_device_ids=true | all-gather | bytes 675840 | tf_op jit(solution)/shard_map/all_gather | solution.py:335
  203.9 0.2 copy.61
  204.1 0.7 copy.75
  204.8 0.2 slice_reduce_fusion
  205.1 0.6 dynamic_slice.18
  205.8 0.6 gather_fusion
  206.4 0.7 select_bitcast_fusion
  207.0 1.2 copy-done.3
  208.2 2.9 %unpack.1 = f32[32,3,16,128]{3,2,1,0:T(8,128)} custom-call(s32[128]{0:T(128)} %source_ref.3, s32[1]{0:T(128)} %bitcast.12.me_ref, f32[64,3,16,128]{3,2,1,0:T(8,128)} %copy-done.3), custom_call_target="tpu_custom_call" | custom-call | tf_op jit(solution)/shard_map/unpack/pallas_call | solution.py:308
  211.1 2.1 copy_bitcast_fusion
  (56 shorter events, 1.2 us)
Async XLA Ops:
  0.6 1.1 copy-start
  0.6 8.6 %copy-start.5 = (f32[8,16,3]{1,0,2:T(8,128)S(1)}, f32[8,16,3]{1,0,2:T(8,128)}, u32[]{:S(2)}) copy-start(f32[8,16,3]{1,0,2:T(8,128)} %param.13) | copy-start | bytes 4612
  0.7 8.5 %copy-start.8 = (f32[16,3]{0,1:T(4,128)S(1)}, f32[16,3]{0,1:T(4,128)}, u32[]{:S(2)}) copy-start(f32[16,3]{0,1:T(4,128)} %param.12) | copy-start | bytes 580
  0.7 8.8 %copy-start.7 = (f32[16]{0:T(128)S(1)}, f32[16]{0:T(128)}, u32[]{:S(2)}) copy-start(f32[16]{0:T(128)} %param.14) | copy-start | bytes 196
  0.7 9.2 %copy-start.10 = (s32[32]{0:T(128)S(1)}, s32[32]{0:T(128)}, u32[]{:S(2)}) copy-start(s32[32]{0:T(128)} %param.18) | copy-start | bytes 388
  0.7 9.3 %copy-start.11 = (f32[16]{0:T(128)S(1)}, f32[16]{0:T(128)}, u32[]{:S(2)}) copy-start(f32[16]{0:T(128)} %param.16) | copy-start | bytes 196
  0.7 9.3 %copy-start.9 = (f32[16]{0:T(128)S(1)}, f32[16]{0:T(128)}, u32[]{:S(2)}) copy-start(f32[16]{0:T(128)} %param.15) | copy-start | bytes 196
  2.7 7.9 %copy-start.6 = (s32[128]{0:T(128)S(1)}, s32[128]{0:T(128)}, u32[]{:S(2)}) copy-start(s32[128]{0:T(128)} %source_ref.3) | copy-start | bytes 1540
  2.7 26.9 %all-to-all-start = ((f32[32,3,16,128]{3,2,1,0:T(8,128)}), f32[32,3,16,128]{3,2,1,0:T(8,128)S(1)}, u32[]{:S(2)}, u32[]{:S(2)}) async-start(f32[32,3,16,128]{3,2,1,0:T(8,128)} %bitcast_bitcast_fusion.1.pos), calls=%async_computation | async-start | bytes 1572864 | tf_op jit(solution)/shard_map/all_to_all | solution.py:225
  74.9 1.2 copy-start.1
  76.1 40.0 %all-to-all-start.1 = ((f32[32,3,16,128]{3,2,1,0:T(8,128)}), f32[32,3,16,128]{3,2,1,0:T(8,128)S(1)}, u32[]{:S(2)}, u32[]{:S(2)}) async-start(f32[32,3,16,128]{3,2,1,0:T(8,128)} %bitcast.13), calls=%async_computation.1 | async-start | bytes 1572864 | tf_op jit(solution)/shard_map/all_to_all | solution.py:292
  79.6 3.0 %copy-start.2 = (f32[4,6,128,128]{3,2,1,0:T(8,128)S(1)}, f32[4,6,128,128]{3,2,1,0:T(8,128)}, u32[]{:S(2)}) copy-start(f32[4,6,128,128]{3,2,1,0:T(8,128)} %copy-done.1) | copy-start | bytes 4718596
  116.1 0.9 copy-start.4
  122.0 85.0 %all-to-all-start.2 = ((f32[64,3,16,128]{3,2,1,0:T(8,128)}), f32[64,3,16,128]{3,2,1,0:T(8,128)S(1)}, u32[]{:S(2)}, u32[]{:S(2)}) async-start(f32[64,3,16,128]{3,2,1,0:T(8,128)} %pack.1), calls=%async_computation.2 | async-start | bytes 3145728 | tf_op jit(solution)/shard_map/all_to_all | solution.py:307
  207.0 1.2 copy-start.3
where the time goes:
time: 214 us; the launch traced here: 213 us
  Pallas kernels  86.1 us (40%)
  blocking collectives  78.1 us (36%)
  waiting for transfers between devices  18.5 us (9%)
  starting transfers between devices  13.7 us (6%)
  local copies, waits for them, and re-layouts  13.3 us (6%)
  other arithmetic  2.46 us (1%)
    all_gather x1, blocking collectives, local(): gathered = lax.all_gather(bundle, ('gx', 'gz', 'gy'), axis=0, tiled=False)  78.1 us
    pallas_call x1, Pallas kernels, local(): pl.pallas_call(functools.partial(pair_kernel, own, sources), grid=(mine,)...  45 us
    pallas_call x2, Pallas kernels, more(): pl.pallas_call(functools.partial(geometry_kernel, start, count, own, sour...  33.1 us
    all_to_all x1, waiting for transfers between devices, local(): lax.all_to_all(pos_blocks, ('gz', 'gy'), split_axis=0, concat_axis=0, til...  18.5 us
    all_to_all x1, starting transfers between devices, local(): lax.all_to_all(pos_blocks, ('gz', 'gy'), split_axis=0, concat_axis=0, til...  6.49 us
    pallas_call x1, Pallas kernels, local(): pl.pallas_call(functools.partial(pack_kernel, blocks_here, capacity), in_...  5.04 us
    unnamed x27, local copies, waits for them, and re-layouts  4.99 us
  transfers between devices with their start and end apart: 3, of which 1 were waited for; matrix products, arithmetic and copies ran while one was open for 4% of the time, Pallas kernels for 16%

commit v1 on v0

--- a/solution.py
+++ b/solution.py
@@ -14,6 +14,7 @@
 TIME_STEP = 0.01
 STEP_ROOT = 0.1
 ROWS = 16
+SCALE = 5.0
 LOG2E = 1.4426950408889634
 
 
@@ -71,65 +72,86 @@
     lax.fori_loop(0, count, geometry, 0)
 
 
-def pair_kernel(own, sources, consts, pos, drift, jgrad, energy, base, twice, shifted, counter, direct):
+def pair_kernel(own, sources, consts, pos, drift, jgrad, energy, base, shifted, counter, direct):
     electrons = own * sources
     lanes = pos.shape[-1]
     groups = electrons // 8
     half = groups // 2
+    tile = math.gcd(half, 4)
+    extent = shifted.shape[2]
     for c in range(3):
         for s in range(sources):
             block = pos[s, 0, c]
             jgrad[0, 3 + c, s * own : (s + 1) * own, :] = block
-            twice[c, s * own : (s + 1) * own, :] = block
-        twice[c, electrons : electrons + 8, :] = twice[c, 0:8, :]
-        for k in range(8):
-            shifted[k, c] = twice[c, k : k + electrons, :]
+            shifted[0, c, s * own : (s + 1) * own, :] = block * SCALE
+        shifted[0, c, electrons:extent, :] = shifted[0, c, 0 : extent - electrons, :]
+        for k in range(1, 8):
+            shifted[k, c, 0 : extent - 8, :] = shifted[0, c, k : k + extent - 8, :]
     counter[...] = jnp.zeros_like(counter)
     direct[...] = jnp.zeros_like(direct)
 
-    def interact(k, i, steps, total):
-        mine = [shifted[0, c, pl.ds(pl.multiple_of(i * 8, 8), 8), :] for c in range(3)]
-        acc = [direct[c, pl.ds(pl.multiple_of(i * 8, 8), 8), :] for c in range(3)]
-        for m in steps:
-            j = lax.rem(i + m, groups)
-            at = pl.ds(pl.multiple_of(j * 8, 8), 8)
-            v = [mine[c] - shifted[k, c, at, :] for c in range(3)]
-            q = (v[0] * v[0] + v[1] * v[1]) + (v[2] * v[2] + SOFT)
-            ri = lax.rsqrt(q)
-            root = lax.rsqrt(1.0 + q * ri)
-            t = root * root
-            t2 = t * t
-            a = t2 * ri
-            total = total + (ri + (t2 * t - a) - (SOFT * (ri * ri)) * (t2 * t + 0.5 * a))
+    def interact(k, first, steps, totals):
+        start = pl.multiple_of(first * 8, 8)
+        mine = [[shifted[0, c, pl.ds(start + 8 * i, 8), :] for c in range(3)] for i in range(tile)]
+        acc = [[direct[c, pl.ds(start + 8 * i, 8), :] for c in range(3)] for i in range(tile)]
+        sum_ri, sum_rest = totals
+        for j in range(steps[0], tile + steps[-1]):
+            at = pl.ds(start + 8 * j, 8)
+            other = [shifted[k, c, at, :] for c in range(3)]
+            back = [counter[k, c, at, :] for c in range(3)]
+            for i in range(tile):
+                if j - i not in steps:
+                    continue
+                v = [mine[i][c] - other[c] for c in range(3)]
+                q = (v[0] * v[0] + v[1] * v[1]) + (v[2] * v[2] + 1.0)
+                ri = lax.rsqrt(q)
+                root = lax.rsqrt(SCALE + q * ri)
+                t = root * root
+                t2 = t * t
+                a = t2 * ri
+                sum_ri = sum_ri + ri
+                sum_rest = sum_rest + t2 * ((t - ri) - (ri * ri) * (t + 0.5 * ri))
+                for c in range(3):
+                    f = a * v[c]
+                    acc[i][c] = acc[i][c] + f
+                    back[c] = back[c] + f
             for c in range(3):
-                f = a * v[c]
-                acc[c] = acc[c] + f
-                counter[k, c, at, :] = counter[k, c, at, :] + f
-        for c in range(3):
-            direct[c, pl.ds(pl.multiple_of(i * 8, 8), 8), :] = acc[c]
-        return total
-
-    total = jnp.zeros((8, lanes), jnp.float32)
-    total = lax.fori_loop(0, groups, lambda i, e: interact(0, i, range(1, half), e), total)
-    total = lax.fori_loop(0, half, lambda i, e: interact(0, i, (half,), e), total)
+                counter[k, c, at, :] = back[c]
+        for i in range(tile):
+            for c in range(3):
+                direct[c, pl.ds(start + 8 * i, 8), :] = acc[i][c]
+        return sum_ri, sum_rest
+
+    tiles = groups // tile
+    zero8 = jnp.zeros((8, lanes), jnp.float32)
+    totals = lax.fori_loop(
+        0, tiles, lambda n, e: interact(0, n * tile, range(1, half), e), (zero8, zero8)
+    )
+    totals = lax.fori_loop(
+        0, half // tile, lambda n, e: interact(0, n * tile, range(half, half + 1), e), totals
+    )
 
     def shifted_groups(n, e):
-        return interact(1 + n // groups, lax.rem(n, groups), range(half), e)
-
-    total = lax.fori_loop(0, 7 * groups, shifted_groups, total)
+        return interact(1 + n // tiles, lax.rem(n, tiles) * tile, range(half), e)
+
+    totals = lax.fori_loop(0, 7 * tiles, shifted_groups, totals)
+    total = SCALE * totals[0] + SCALE**3 * totals[1]
     square = jnp.zeros((electrons, lanes), jnp.float32)
     for c in range(3):
-        back = counter[0, c]
-        for k in range(1, 8):
-            back = back + pltpu.roll(counter[k, c], k, 0)
-        value = 0.5 * (direct[c] - back)
+        back = None
+        for k in range(8):
+            counter[k, c, 0 : extent - electrons, :] = (
+                counter[k, c, 0 : extent - electrons, :] + counter[k, c, electrons:extent, :]
+            )
+            part = counter[k, c, 0:electrons, :]
+            back = part if k == 0 else back + pltpu.roll(part, k, 0)
+        value = 0.5 * SCALE**2 * (direct[c] - back)
         jgrad[0, c] = value
         square = square + value * value
     base[0] = jnp.broadcast_to(
         jnp.sum(total, axis=0, keepdims=True) - 0.5 * jnp.sum(square, axis=0, keepdims=True),
         (8, lanes),
     )
-    e_sum = jnp.zeros((1, lanes), jnp.float32)
 
     def slab(n, e_sum):
         at = pl.ds(pl.multiple_of(n * own, own), own)
@@ -183,6 +205,69 @@
         return carry
 
     lax.fori_loop(0, blocks_here, one, 0)
+
+
+def exchange_kernel(group_in, all_in, group_out, all_out, group_send, group_recv, all_send, all_recv):
+    nz, nx, ny = lax.axis_size("gz"), lax.axis_size("gx"), lax.axis_size("gy")
+    z, x, y = lax.axis_index("gz"), lax.axis_index("gx"), lax.axis_index("gy")
+    group = nz * ny
+    me_in_group = z * ny + y
+    me = x * group + me_in_group
+
+    def target(offset):
+        dx, rest = offset // group, offset % group
+        return (
+            lax.rem(z + rest // ny, nz),
+            lax.rem(x + dx, nx),
+            lax.rem(y + rest % ny, ny),
+        )
+
+    def where(offset):
+        tz, tx, ty = target(offset)
+        return {"gz": tz, "gx": tx, "gy": ty}
+
+    def all_copy(offset):
+        return pltpu.make_async_remote_copy(
+            src_ref=all_in,
+            dst_ref=all_out.at[me],
+            send_sem=all_send.at[offset],
+            recv_sem=all_recv.at[offset],
+            device_id=where(offset),
+            device_id_type=pl.DeviceIdType.MESH,
+        )
+
+    def group_copy(offset):
+        return pltpu.make_async_remote_copy(
+            src_ref=group_in.at[target(offset)[0]],
+            dst_ref=group_out.at[me_in_group],
+            send_sem=group_send.at[offset],
+            recv_sem=group_recv.at[offset],
+            device_id=where(offset),
+            device_id_type=pl.DeviceIdType.MESH,
+        )
+
+    def loop(first, last, step):
+        def body(n, carry):
+            step(n)
+            return carry
+
+        lax.fori_loop(first, last, body, 0)
+
+    barrier = pltpu.get_barrier_semaphore()
+    loop(
+        1,
+        nx * group,
+        lambda n: pl.semaphore_signal(
+            barrier, inc=1, device_id=where(n), device_id_type=pl.DeviceIdType.MESH
+        ),
+    )
+    pl.semaphore_wait(barrier, nx * group - 1)
+    loop(1, group, lambda n: group_copy(n).start())
+    loop(1, nx * group, lambda n: all_copy(n).start())
+    group_out[me_in_group] = group_in[z]
+    all_out[me] = all_in[...]
+    loop(1, group, lambda n: group_copy(n).wait())
+    loop(1, nx * group, lambda n: all_copy(n).wait())
 
 
 def nuclear_repulsion(centers, charges):
@@ -261,9 +346,8 @@
             lane_shape,
         ],
         scratch_shapes=[
-            pltpu.VMEM((3, electrons + 8, BLK), jnp.float32),
-            pltpu.VMEM((8, 3, electrons, BLK), jnp.float32),
-            pltpu.VMEM((8, 3, electrons, BLK), jnp.float32),
+            pltpu.VMEM((8, 3, electrons + electrons // 2 + 8, BLK), jnp.float32),
+            pltpu.VMEM((8, 3, electrons + electrons // 2 + 8, BLK), jnp.float32),
             pltpu.VMEM((3, electrons, BLK), jnp.float32),
         ],
         compiler_params=pltpu.CompilerParams(vmem_limit_bytes=32 * 2**20),
@@ -271,7 +355,7 @@
         name="pairs",
     )(table, arrived)
 
-    def more(start, count):
+    def more(start, count, jgrad):
         return pl.pallas_call(
             functools.partial(geometry_kernel, start, count, own, sources),
             grid=(mine,),
@@ -286,8 +370,7 @@
         )(table, arrived, jgrad)
 
     split = max(1, (geometries - 1) // 2)
-    energy_a, log_a = more(1, split)
-    energy_b, log_b = more(1 + split, geometries - 1 - split)
+    energy_a, log_a = more(1, split, jgrad)
 
     drift_back = lax.all_to_all(
         drift.reshape(blocks_here, 3, own, BLK), ("gz", "gy"), split_axis=0, concat_axis=0, tiled=True
@@ -304,6 +387,8 @@
         scratch_shapes=[pltpu.SMEM((peers,), jnp.int32)],
         name="pack",
     )(branch_source, me, pos_blocks, drift_back, noise_blocks)
+    jgrad_later, sent = lax.optimization_barrier((jgrad, sent))
+    energy_b, log_b = more(1 + split, geometries - 1 - split, jgrad_later)
     received = lax.all_to_all(sent, "gx", split_axis=0, concat_axis=0, tiled=True)
     new_blocks = pl.pallas_call(
         functools.partial(unpack_kernel, blocks_here, capacity),
@@ -330,20 +415,40 @@
     ).astype(jnp.float32)
     omega = alive_weights[:, None, :] * jnp.exp(2.0 * (log_sums - log_sums[:, 0:1]))
     sums = jnp.concatenate([jnp.sum(omega * energies, axis=(0, 2)), jnp.sum(omega, axis=(0, 2))])
-    sums = jnp.pad(sums, (0, local_walkers - 2 * geometries)).reshape(mine, 1, BLK)
-    bundle = jnp.concatenate([energies, alive_weights[:, None, :], sums], axis=1)
-    gathered = lax.all_gather(bundle, ("gx", "gz", "gy"), axis=0, tiled=False)
+    sums = jnp.pad(sums, (0, local_walkers - 2 * geometries)).reshape(mine, BLK)
+    rows = energies.transpose(1, 0, 2)
+    replicas = lax.axis_size("gz")
+    for_group = rows.reshape(replicas, per_replica * mine, BLK)
+    for_all = jnp.concatenate([rows[0], alive_weights, sums, sums], axis=0)
+    group_rows, all_rows = pl.pallas_call(
+        exchange_kernel,
+        in_specs=[vmem, vmem],
+        out_specs=[vmem, vmem],
+        out_shape=[
+            jax.ShapeDtypeStruct((sources, per_replica * mine, BLK), jnp.float32),
+            jax.ShapeDtypeStruct((peers * sources, 4 * mine, BLK), jnp.float32),
+        ],
+        scratch_shapes=[
+            pltpu.SemaphoreType.DMA((sources,)),
+            pltpu.SemaphoreType.DMA((sources,)),
+            pltpu.SemaphoreType.DMA((peers * sources,)),
+            pltpu.SemaphoreType.DMA((peers * sources,)),
+        ],
+        compiler_params=pltpu.CompilerParams(collective_id=0, has_side_effects=True),
+        name="exchange",
+    )(for_group, for_all)
+    all_rows = all_rows.reshape(peers * sources, 4, mine, BLK)
     total = jnp.sum(
-        gathered[:, :, geometries + 1, :].reshape(-1, local_walkers)[:, : 2 * geometries], axis=0
+        all_rows[:, 2].reshape(peers * sources, local_walkers)[:, : 2 * geometries], axis=0
     )
     estimate = total[:geometries] / total[geometries:]
     first_geometry = lax.axis_index("gz") * per_replica
-    rows = gathered.reshape(peers, sources * mine, geometries + 2, BLK)
-    ours = lax.dynamic_slice(
-        rows, (device, 0, first_geometry, 0), (1, sources * mine, per_replica, BLK)
-    )
-    local_energy = ours[0].transpose(1, 0, 2).reshape(per_replica, walkers)
-    kept = rows[:, :, geometries, :] * jnp.exp(estimate[0] - rows[:, :, 0, :])
+    local_energy = (
+        group_rows.reshape(sources, per_replica, local_walkers)
+        .transpose(1, 0, 2)
+        .reshape(per_replica, walkers)
+    )
+    kept = all_rows[:, 1] * jnp.exp(estimate[0] - all_rows[:, 0])
     kept = kept.reshape(peers * blocks_here, BLK)
     my_sources = lax.dynamic_slice_in_dim(branch_source, device * blocks_here, blocks_here, 0)
     new_weights = jnp.take(kept, my_sources, axis=0).reshape(walkers)

time: 214 us -> 142 us (0.66)
  blocking collectives: 78.1 us -> 0 us
  waiting for transfers between devices: 18.5 us -> 21.6 us
    all_gather x1 -> x0, blocking collectives: 78.1 us -> none  [local(): gathered = lax.all_gather(bundle, ('gx', 'gz', 'gy'), axis=0, tiled=False)]
    pallas_call x1, Pallas kernels: 45 us -> 28.6 us  [local(): pl.pallas_call(functools.partial(pair_kernel, own, sources), grid=(mine,)...]
    pallas_call x0 -> x1, Pallas kernels: none -> 15.6 us  [local(): pl.pallas_call(exchange_kernel, in_specs=[vmem, vmem], out_specs=[vmem, v...]
    all_to_all x1, waiting for transfers between devices: 0.01 us -> 2.79 us  [local(): lax.all_to_all(drift.reshape(blocks_here, 3, own, BLK), ('gz', 'gy'), spl...]
    unnamed x27 -> x31, local copies, waits for them, and re-layouts: 4.99 us -> 4.61 us
  transfers between devices with their start and end apart: 3 -> 3, of which waited for: 1 -> 2; matrix products, arithmetic and copies ran while one was open for 4% -> 8% of each run, Pallas kernels for 16% -> 35%
where the time goes in v1:
time: 142 us; the launch traced here: 141 us
  Pallas kernels  85.2 us (60%)
  waiting for transfers between devices  21.6 us (15%)
  local copies, waits for them, and re-layouts  14.8 us (10%)
  starting transfers between devices  14.4 us (10%)
  other arithmetic  3.97 us (3%)
    pallas_call x2, Pallas kernels, more(): pl.pallas_call(functools.partial(geometry_kernel, start, count, own, sour...  33.1 us
    pallas_call x1, Pallas kernels, local(): pl.pallas_call(functools.partial(pair_kernel, own, sources), grid=(mine,)...  28.6 us
    all_to_all x1, waiting for transfers between devices, local(): lax.all_to_all(pos_blocks, ('gz', 'gy'), split_axis=0, concat_axis=0, til...  18.8 us
    pallas_call x1, Pallas kernels, local(): pl.pallas_call(exchange_kernel, in_specs=[vmem, vmem], out_specs=[vmem, v...  15.6 us
    all_to_all x1, starting transfers between devices, local(): lax.all_to_all(pos_blocks, ('gz', 'gy'), split_axis=0, concat_axis=0, til...  6.49 us
    pallas_call x1, Pallas kernels, local(): pl.pallas_call(functools.partial(pack_kernel, blocks_here, capacity), in_...  5.03 us
    unnamed x31, local copies, waits for them, and re-layouts  4.61 us
    all_to_all x1, starting transfers between devices, local(): lax.all_to_all(sent, 'gx', split_axis=0, concat_axis=0, tiled=True)  4.36 us
  transfers between devices with their start and end apart: 3, of which 2 were waited for; matrix products, arithmetic and copies ran while one was open for 8% of the time, Pallas kernels for 35%

profile of v1, /device:TPU:0, one launch (start us, length us, event | category | flops | bytes accessed | tf_op | source)
XLA Modules:
  0.0 140.9 jit_solution(3437610762104690144)
XLA Ops:
  0.7 1.1 copy-done
  1.8 0.9 bitcast_bitcast_fusion.1.pos
  2.7 6.5 %all-to-all-start = ((f32[32,3,16,128]{3,2,1,0:T(8,128)}), f32[32,3,16,128]{3,2,1,0:T(8,128)S(1)}, u32[]{:S(2)}, u32[]{:S(2)}) async-start(f32[32,3,16,128]{3,2,1,0:T(8,128)} %bitcast_bitcast_fusion.1.pos), calls=%async_computation | async-start | bytes 1572864 | tf_op jit(solution)/shard_map/all_to_all | solution.py:310
  9.2 0.1 copy.45
  9.5 0.1 copy.46
  10.3 0.2 stack.12
  10.8 18.8 %all-to-all-done = f32[32,3,16,128]{3,2,1,0:T(8,128)S(1)} async-done(((f32[32,3,16,128]{3,2,1,0:T(8,128)}), f32[32,3,16,128]{3,2,1,0:T(8,128)S(1)}, u32[]{:S(2)}, u32[]{:S(2)}) %all-to-all-start) | async-done | bytes 786464 | tf_op jit(solution)/shard_map/all_to_all | solution.py:310
  29.6 0.3 broadcast_in_dim.11.consts
  29.9 28.6 %pairs.1 = (f32[8,4,3,16,128]{4,3,2,1,0:T(8,128)}, f32[4,6,128,128]{3,2,1,0:T(8,128)S(1)}, f32[4,8,128]{2,1,0:T(8,128)S(1)}, f32[4,8,128]{2,1,0:T(8,128)S(1)}) custom-call(f32[8,16,16,128]{3,2,1,0:T(8,128)S(1)} %broadcast_in_dim.11.consts, f32[8,4,3,16,128]{4,3,2,1,0:T(8,128)S(1)} %bitcast.50), custom_call_target="tpu_custom_call" | custom-call | flops 100000000 | bytes 4000000 | tf_op jit(solution)/shard_map/pairs/pallas_call | solution.py:337
  58.5 1.2 copy-done.1
  59.6 3.5 %all-to-all-start.1 = ((f32[32,3,16,128]{3,2,1,0:T(8,128)}), f32[32,3,16,128]{3,2,1,0:T(8,128)S(1)}, u32[]{:S(2)}, u32[]{:S(2)}) async-start(f32[32,3,16,128]{3,2,1,0:T(8,128)} %bitcast.4), calls=%async_computation.1 | async-start | bytes 1572864 | tf_op jit(solution)/shard_map/all_to_all | solution.py:375
  63.3 0.2 multiply_reduce_fusion.1
  63.5 0.9 dynamic-slice_select_fusion
  64.3 2.1 %bitcast_bitcast_fusion.noise = f32[32,3,16,128]{3,2,1,0:T(8,128)} fusion(f32[16,3,4096]{2,0,1:T(8,128)} %param.11), kind=kLoop, calls=%fused_computation.2 | loop fusion | bytes 1572864 | tf_op jit(solution)/shard_map/transpose | solution.py:306
  66.5 14.2 %geometries_1.1 = (f32[4,8,128]{2,1,0:T(8,128)S(1)}, f32[4,8,128]{2,1,0:T(8,128)S(1)}) custom-call(f32[8,16,16,128]{3,2,1,0:T(8,128)S(1)} %broadcast_in_dim.11.consts, f32[8,4,3,16,128]{4,3,2,1,0:T(8,128)S(1)} %bitcast.51, f32[4,6,128,128]{3,2,1,0:T(8,128)S(1)} %copy-done.2), custom_call_target="tpu_custom_call" | custom-call | flops 90000000 | bytes 8000000 | tf_op jit(solution)/shard_map/geometries_1/pallas_call | solution.py:359
  80.7 2.8 %all-to-all-done.1.drift = f32[32,3,16,128]{3,2,1,0:T(8,128)S(1)} async-done(((f32[32,3,16,128]{3,2,1,0:T(8,128)}), f32[32,3,16,128]{3,2,1,0:T(8,128)S(1)}, u32[]{:S(2)}, u32[]{:S(2)}) %all-to-all-start.1) | async-done | bytes 786464 | tf_op jit(solution)/shard_map/all_to_all | solution.py:375
  83.5 0.9 copy-done.4
  84.5 5.0 %pack.1 = f32[64,3,16,128]{3,2,1,0:T(8,128)} custom-call(s32[128]{0:T(128)} %source_ref.3, s32[1]{0:T(128)} %bitcast.3.me_ref, f32[32,3,16,128]{3,2,1,0:T(8,128)} %bitcast_bitcast_fusion.1.pos, f32[32,3,16,128]{3,2,1,0:T(8,128)} %copy-done.4, f32[32,3,16,128]{3,2,1,0:T(8,128)} %bitcast_bitcast_fusion.noise), custom_call_target="tpu_custom_call" | custom-call | tf_op jit(solution)/shard_map/pack/pallas_call | solution.py:382
  89.5 4.4 %all-to-all-start.2 = ((f32[64,3,16,128]{3,2,1,0:T(8,128)}), f32[64,3,16,128]{3,2,1,0:T(8,128)}, u32[]{:S(2)}, u32[]{:S(2)}) async-start(f32[64,3,16,128]{3,2,1,0:T(8,128)} %pack.1), calls=%async_computation.2 | async-start | bytes 3145728 | tf_op jit(solution)/shard_map/all_to_all | solution.py:392
  93.9 1.4 copy-done.3
  95.3 18.9 %geometries_4.1 = (f32[4,8,128]{2,1,0:T(8,128)S(1)}, f32[4,8,128]{2,1,0:T(8,128)S(1)}) custom-call(f32[8,16,16,128]{3,2,1,0:T(8,128)S(1)} %broadcast_in_dim.11.consts, f32[8,4,3,16,128]{4,3,2,1,0:T(8,128)S(1)} %bitcast.52, f32[4,6,128,128]{3,2,1,0:T(8,128)S(1)} %copy-done.3), custom_call_target="tpu_custom_call" | custom-call | flops 120000000 | bytes 8000000 | tf_op jit(solution)/shard_map/geometries_4/pallas_call | solution.py:359
  114.2 0.2 multiply_reduce_fusion.2
  114.5 0.6 pad_maximum_fusion.all_in
  115.2 15.6 %exchange.1 = (f32[8,16,128]{2,1,0:T(8,128)}, f32[32,16,128]{2,1,0:T(8,128)}) custom-call(f32[2,16,128]{2,1,0:T(8,128)} %bitcast.59, f32[16,128]{1,0:T(8,128)} %pad_maximum_fusion.all_in), custom_call_target="tpu_custom_call" | custom-call | tf_op jit(solution)/shard_map/exchange/pallas_call | solution.py:423
  130.7 1.5 %reshape.128 = f32[8,4,512]{2,1,0:T(4,128)} reshape(f32[8,16,128]{2,1,0:T(8,128)} %get-tuple-element.25) | data formatting | bytes 131072 | tf_op jit(solution)/shard_map/reshape | solution.py:447
  132.2 0.8 slice.88
  133.2 0.6 dynamic_slice.14
  133.8 0.9 fusion.1
  134.7 0.6 gather_fusion
  135.3 0.7 select_bitcast_fusion
  136.0 2.9 %unpack.1 = f32[32,3,16,128]{3,2,1,0:T(8,128)} custom-call(s32[128]{0:T(128)} %source_ref.3, s32[1]{0:T(128)} %bitcast.3.me_ref, f32[64,3,16,128]{3,2,1,0:T(8,128)} %all-to-all-done.2.received), custom_call_target="tpu_custom_call" | custom-call | tf_op jit(solution)/shard_map/unpack/pallas_call | solution.py:393
  138.9 2.1 %copy_bitcast_fusion = f32[16,3,4096]{2,0,1:T(8,128)} fusion(f32[32,3,16,128]{3,2,1,0:T(8,128)} %unpack.1), kind=kLoop, calls=%fused_computation.1 | loop fusion | bytes 1572864 | tf_op jit(solution)/shard_map/reshape | solution.py:401
  (68 shorter events, 1.4 us)
Async XLA Ops:
  0.6 1.1 copy-start
  0.6 8.6 %copy-start.8 = (f32[8,16,3]{1,0,2:T(8,128)S(1)}, f32[8,16,3]{1,0,2:T(8,128)}, u32[]{:S(2)}) copy-start(f32[8,16,3]{1,0,2:T(8,128)} %param.13) | copy-start | bytes 4612
  0.7 8.5 %copy-start.11 = (f32[16,3]{0,1:T(4,128)S(1)}, f32[16,3]{0,1:T(4,128)}, u32[]{:S(2)}) copy-start(f32[16,3]{0,1:T(4,128)} %param.12) | copy-start | bytes 580
  0.7 8.7 %copy-start.10 = (f32[16]{0:T(128)S(1)}, f32[16]{0:T(128)}, u32[]{:S(2)}) copy-start(f32[16]{0:T(128)} %param.14) | copy-start | bytes 196
  0.7 9.2 %copy-start.13 = (s32[32]{0:T(128)S(1)}, s32[32]{0:T(128)}, u32[]{:S(2)}) copy-start(s32[32]{0:T(128)} %param.18) | copy-start | bytes 388
  0.7 9.3 %copy-start.14 = (f32[16]{0:T(128)S(1)}, f32[16]{0:T(128)}, u32[]{:S(2)}) copy-start(f32[16]{0:T(128)} %param.16) | copy-start | bytes 196
  0.7 9.3 %copy-start.12 = (f32[16]{0:T(128)S(1)}, f32[16]{0:T(128)}, u32[]{:S(2)}) copy-start(f32[16]{0:T(128)} %param.15) | copy-start | bytes 196
  2.7 7.9 %copy-start.9 = (s32[128]{0:T(128)S(1)}, s32[128]{0:T(128)}, u32[]{:S(2)}) copy-start(s32[128]{0:T(128)} %source_ref.3) | copy-start | bytes 1540
  2.7 26.9 %all-to-all-start = ((f32[32,3,16,128]{3,2,1,0:T(8,128)}), f32[32,3,16,128]{3,2,1,0:T(8,128)S(1)}, u32[]{:S(2)}, u32[]{:S(2)}) async-start(f32[32,3,16,128]{3,2,1,0:T(8,128)} %bitcast_bitcast_fusion.1.pos), calls=%async_computation | async-start | bytes 1572864 | tf_op jit(solution)/shard_map/all_to_all | solution.py:310
  58.5 1.2 copy-start.1
  59.6 23.9 %all-to-all-start.1 = ((f32[32,3,16,128]{3,2,1,0:T(8,128)}), f32[32,3,16,128]{3,2,1,0:T(8,128)S(1)}, u32[]{:S(2)}, u32[]{:S(2)}) async-start(f32[32,3,16,128]{3,2,1,0:T(8,128)} %bitcast.4), calls=%async_computation.1 | async-start | bytes 1572864 | tf_op jit(solution)/shard_map/all_to_all | solution.py:375
  63.2 3.3 %copy-start.2 = (f32[4,6,128,128]{3,2,1,0:T(8,128)S(1)}, f32[4,6,128,128]{3,2,1,0:T(8,128)}, u32[]{:S(2)}) copy-start(f32[4,6,128,128]{3,2,1,0:T(8,128)} %copy-done.1) | copy-start | bytes 4718596
  80.7 8.8 %copy-start.6 = (f32[4,8,128]{2,0,1:T(4,128)}, f32[4,8,128]{2,0,1:T(4,128)S(1)}, u32[]{:S(2)}) copy-start(f32[4,8,128]{2,0,1:T(4,128)S(1)} %copy.52) | copy-start | bytes 49156
  80.7 8.8 %copy-start.7 = (f32[4,8,128]{2,0,1:T(4,128)}, f32[4,8,128]{2,0,1:T(4,128)S(1)}, u32[]{:S(2)}) copy-start(f32[4,8,128]{2,0,1:T(4,128)S(1)} %copy.58) | copy-start | bytes 49156
  83.5 0.9 copy-start.4
  89.5 46.5 %all-to-all-start.2 = ((f32[64,3,16,128]{3,2,1,0:T(8,128)}), f32[64,3,16,128]{3,2,1,0:T(8,128)}, u32[]{:S(2)}, u32[]{:S(2)}) async-start(f32[64,3,16,128]{3,2,1,0:T(8,128)} %pack.1), calls=%async_computation.2 | async-start | bytes 3145728 | tf_op jit(solution)/shard_map/all_to_all | solution.py:392
  93.9 1.4 copy-start.3
  95.3 19.0 %slice-start = ((f32[4,8,128]{2,0,1:T(4,128)}), f32[4,3,128]{2,0,1:T(4,128)S(1)}, s32[]{:S(2)}) async-start(f32[4,8,128]{2,0,1:T(4,128)} %copy-done.6), calls=%async_computation.3 | async-start | bytes 12288 | tf_op jit(solution)/shard_map/slice | solution.py:404
  95.3 19.0 %slice-start.1 = ((f32[4,8,128]{2,0,1:T(4,128)}), f32[4,3,128]{2,0,1:T(4,128)S(1)}, s32[]{:S(2)}) async-start(f32[4,8,128]{2,0,1:T(4,128)} %copy-done.7), calls=%async_computation.4 | async-start | bytes 12288 | tf_op jit(solution)/shard_map/slice | solution.py:407
  114.5 0.7 copy-start.5

commit v2 on v1

--- a/solution.py
+++ b/solution.py
@@ -49,9 +49,8 @@
     return jnp.log(phi), grad, lap, pot
 
 
-def geometry_kernel(first, count, own, sources, consts, pos, jgrad, energy, logs):
-    electrons = own * sources
-    lanes = pos.shape[-1]
+def geometry_kernel(first, count, electrons, consts, jgrad, energy, logs):
+    lanes = jgrad.shape[-1]
 
     def geometry(step, carry):
         g = first + step
@@ -72,7 +71,8 @@
     lax.fori_loop(0, count, geometry, 0)
 
 
-def pair_kernel(own, sources, consts, pos, drift, jgrad, energy, base, shifted, counter, direct):
+def pair_kernel(own, sources, consts, pos, *refs):
+    drift, jgrad, energy, base, shifted, counter, direct = refs[-7:]
     electrons = own * sources
     lanes = pos.shape[-1]
     groups = electrons // 8
@@ -207,67 +207,99 @@
     lax.fori_loop(0, blocks_here, one, 0)
 
 
-def exchange_kernel(group_in, all_in, group_out, all_out, group_send, group_recv, all_send, all_recv):
+def exchange_kernel(
+    geometries,
+    mine,
+    source_ref,
+    group_in,
+    all_in,
+    energy_out,
+    estimate_out,
+    weight_out,
+    group_out,
+    all_out,
+    group_send,
+    group_recv,
+    all_send,
+    all_recv,
+):
     nz, nx, ny = lax.axis_size("gz"), lax.axis_size("gx"), lax.axis_size("gy")
     z, x, y = lax.axis_index("gz"), lax.axis_index("gx"), lax.axis_index("gy")
     group = nz * ny
     me_in_group = z * ny + y
     me = x * group + me_in_group
-
-    def target(offset):
+    blocks_here = group * mine
+
+    def shifted_index(index, by, size):
+        return index if by == 0 else lax.rem(index + by, size)
+
+    def where(offset):
         dx, rest = offset // group, offset % group
-        return (
-            lax.rem(z + rest // ny, nz),
-            lax.rem(x + dx, nx),
-            lax.rem(y + rest % ny, ny),
+        return {
+            "gz": shifted_index(z, rest // ny, nz),
+            "gx": shifted_index(x, dx, nx),
+            "gy": shifted_index(y, rest % ny, ny),
+        }
+
+    barrier = pltpu.get_barrier_semaphore()
+    for n in range(1, nx * group):
+        pl.semaphore_signal(
+            barrier, inc=1, device_id=where(n), device_id_type=pl.DeviceIdType.MESH
         )
-
-    def where(offset):
-        tz, tx, ty = target(offset)
-        return {"gz": tz, "gx": tx, "gy": ty}
-
-    def all_copy(offset):
-        return pltpu.make_async_remote_copy(
-            src_ref=all_in,
-            dst_ref=all_out.at[me],
-            send_sem=all_send.at[offset],
-            recv_sem=all_recv.at[offset],
-            device_id=where(offset),
-            device_id_type=pl.DeviceIdType.MESH,
+    pl.semaphore_wait(barrier, nx * group - 1)
+    copies = []
+    for n in range(1, nx * group):
+        copies.append(
+            pltpu.make_async_remote_copy(
+                src_ref=all_in,
+                dst_ref=all_out.at[me],
+                send_sem=all_send.at[n],
+                recv_sem=all_recv.at[n],
+                device_id=where(n),
+                device_id_type=pl.DeviceIdType.MESH,
+            )
         )
-
-    def group_copy(offset):
-        return pltpu.make_async_remote_copy(
-            src_ref=group_in.at[target(offset)[0]],
-            dst_ref=group_out.at[me_in_group],
-            send_sem=group_send.at[offset],
-            recv_sem=group_recv.at[offset],
-            device_id=where(offset),
-            device_id_type=pl.DeviceIdType.MESH,
+        copies[-1].start()
+    for n in range(1, group):
+        target = where(n)
+        copies.append(
+            pltpu.make_async_remote_copy(
+                src_ref=group_in.at[target["gz"]],
+                dst_ref=group_out.at[me_in_group],
+                send_sem=group_send.at[n],
+                recv_sem=group_recv.at[n],
+                device_id=target,
+                device_id_type=pl.DeviceIdType.MESH,
+            )
         )
-
-    def loop(first, last, step):
-        def body(n, carry):
-            step(n)
-            return carry
-
-        lax.fori_loop(first, last, body, 0)
-
-    barrier = pltpu.get_barrier_semaphore()
-    loop(
-        1,
-        nx * group,
-        lambda n: pl.semaphore_signal(
-            barrier, inc=1, device_id=where(n), device_id_type=pl.DeviceIdType.MESH
-        ),
-    )
-    pl.semaphore_wait(barrier, nx * group - 1)
-    loop(1, group, lambda n: group_copy(n).start())
-    loop(1, nx * group, lambda n: all_copy(n).start())
+        copies[-1].start()
     group_out[me_in_group] = group_in[z]
     all_out[me] = all_in[...]
-    loop(1, group, lambda n: group_copy(n).wait())
-    loop(1, nx * group, lambda n: all_copy(n).wait())
+    for copy in copies:
+        copy.wait()
+
+    total = jnp.sum(all_out[:, 2 * mine : 4 * mine, :], axis=0)
+    total = jnp.broadcast_to(total[0:1], (8, BLK))
+    below = lax.broadcasted_iota(jnp.int32, (8, BLK), 1) < geometries
+    weight_total = jnp.where(below, pltpu.roll(total, BLK - geometries, 1), 1.0)
+    estimate = total / weight_total
+    estimate_out[...] = estimate
+    reference_estimate = estimate[0:1, 0:1]
+
+    def one(d, carry):
+        source = source_ref[x * blocks_here + d]
+        holder, block = source // mine, source % mine
+        energy = all_out[holder, pl.ds(block, 1), :]
+        alive = all_out[holder, pl.ds(mine + block, 1), :]
+        weight_out[pl.ds(d, 1), :] = alive * jnp.exp(reference_estimate - energy)
+        return carry
+
+    lax.fori_loop(0, blocks_here, one, 0)
+    per = energy_out.shape[0]
+    for p in range(group):
+        for b in range(mine):
+            lanes = slice((p * mine + b) * BLK, (p * mine + b + 1) * BLK)
+            energy_out[:, lanes] = group_out[p, b * per : (b + 1) * per, :]
 
 
 def nuclear_repulsion(centers, charges):
@@ -307,8 +339,14 @@
 
     pos_blocks = to_blocks(positions)
     noise_blocks = to_blocks(diffusion_noise)
-    arrived = lax.all_to_all(pos_blocks, ("gz", "gy"), split_axis=0, concat_axis=0, tiled=True)
-    arrived = arrived.reshape(sources, mine, 3, own, BLK)
+    early = 1 if mine > 1 else mine
+    by_device = pos_blocks.reshape(sources, mine, 3, own, BLK)
+
+    def spread(x):
+        return lax.all_to_all(x, ("gz", "gy"), split_axis=0, concat_axis=0, tiled=True)
+
+    arrived = spread(by_device[:, :early])
+    arrived_later = spread(by_device[:, early:]) if early < mine else None
 
     centers = base_nuclei[None, :, :] + displacements
     shape = (geometries, NA)
@@ -332,45 +370,74 @@
     table_spec = pl.BlockSpec(table.shape, lambda b: (0, 0, 0, 0))
     pos_spec = pl.BlockSpec((sources, 1, 3, own, BLK), lambda b: (0, b, 0, 0, 0))
     grad_spec = pl.BlockSpec((1, 6, electrons, BLK), lambda b: (b, 0, 0, 0))
-    lane_shape = jax.ShapeDtypeStruct((mine, 8, BLK), jnp.float32)
-    grad_shape = jax.ShapeDtypeStruct((mine, 6, electrons, BLK), jnp.float32)
-    drift, jgrad, first, base = pl.pallas_call(
-        functools.partial(pair_kernel, own, sources),
-        grid=(mine,),
-        in_specs=[table_spec, pos_spec],
-        out_specs=[pos_spec, grad_spec, lane_spec, lane_spec],
-        out_shape=[
-            jax.ShapeDtypeStruct(arrived.shape, jnp.float32),
-            grad_shape,
-            lane_shape,
-            lane_shape,
-        ],
-        scratch_shapes=[
-            pltpu.VMEM((8, 3, electrons + electrons // 2 + 8, BLK), jnp.float32),
-            pltpu.VMEM((8, 3, electrons + electrons // 2 + 8, BLK), jnp.float32),
-            pltpu.VMEM((3, electrons, BLK), jnp.float32),
-        ],
-        compiler_params=pltpu.CompilerParams(vmem_limit_bytes=32 * 2**20),
-        cost_estimate=pl.CostEstimate(flops=100_000_000, bytes_accessed=4_000_000, transcendentals=0),
-        name="pairs",
-    )(table, arrived)
+    extent = electrons + electrons // 2 + 8
+
+    def pairs(coords, start, *previous):
+        blocks = coords.shape[1]
+        lane_shape = jax.ShapeDtypeStruct((blocks, 8, BLK), jnp.float32)
+        return pl.pallas_call(
+            functools.partial(pair_kernel, own, sources),
+            grid=(blocks,),
+            in_specs=[table_spec, pos_spec] + [pl.BlockSpec(memory_space=pl.ANY)] * len(previous),
+            out_specs=[
+                pl.BlockSpec((sources, 1, 3, own, BLK), lambda b: (0, b + start, 0, 0, 0)),
+                grad_spec,
+                lane_spec,
+                lane_spec,
+            ],
+            out_shape=[
+                jax.ShapeDtypeStruct((sources, mine, 3, own, BLK), jnp.float32),
+                jax.ShapeDtypeStruct((blocks, 6, electrons, BLK), jnp.float32),
+                lane_shape,
+                lane_shape,
+            ],
+            scratch_shapes=[
+                pltpu.VMEM((8, 3, extent, BLK), jnp.float32),
+                pltpu.VMEM((8, 3, extent, BLK), jnp.float32),
+                pltpu.VMEM((3, electrons, BLK), jnp.float32),
+            ],
+            input_output_aliases={2: 0} if previous else {},
+            compiler_params=pltpu.CompilerParams(vmem_limit_bytes=32 * 2**20),
+            cost_estimate=pl.CostEstimate(
+                flops=blocks * 25_000_000, bytes_accessed=blocks * 1_000_000, transcendentals=0
+            ),
+            name=f"pairs_{start}",
+        )(table, coords, *previous)
 
     def more(start, count, jgrad):
-        return pl.pallas_call(
-            functools.partial(geometry_kernel, start, count, own, sources),
-            grid=(mine,),
-            in_specs=[table_spec, pos_spec, grad_spec],
+        blocks = jgrad.shape[0]
+        lane_shape = jax.ShapeDtypeStruct((blocks, 8, BLK), jnp.float32)
+        energy, logs = pl.pallas_call(
+            functools.partial(geometry_kernel, start, count, electrons),
+            grid=(blocks,),
+            in_specs=[table_spec, grad_spec],
             out_specs=[lane_spec, lane_spec],
             out_shape=[lane_shape, lane_shape],
             compiler_params=pltpu.CompilerParams(vmem_limit_bytes=16 * 2**20),
             cost_estimate=pl.CostEstimate(
-                flops=count * 30_000_000, bytes_accessed=8_000_000, transcendentals=0
+                flops=blocks * count * 7_500_000,
+                bytes_accessed=blocks * 2_000_000,
+                transcendentals=0,
             ),
-            name=f"geometries_{start}",
-        )(table, arrived, jgrad)
-
-    split = max(1, (geometries - 1) // 2)
-    energy_a, log_a = more(1, split, jgrad)
+            name=f"geometries_{start}_{blocks}",
+        )(table, jgrad)
+        return energy[:, :count], logs[:, :count]
+
+    split = max(1, geometries // 2)
+    drift, jgrad, first, base = pairs(arrived, 0)
+    if arrived_later is None:
+        energy_a, log_a = more(1, split, jgrad)
+        early_rows = None
+    else:
+        early_energy, early_log = more(1, geometries - 1, jgrad)
+        early_rows = (
+            jnp.concatenate([first[:, 0:1], early_energy], axis=1),
+            jnp.concatenate([first[:, 1:2], early_log], axis=1),
+            base,
+        )
+        arrived_later, early_rows = lax.optimization_barrier((arrived_later, early_rows))
+        drift, jgrad, first, base = pairs(arrived_later, early, drift)
+        energy_a, log_a = more(1, split, jgrad)
 
     drift_back = lax.all_to_all(
         drift.reshape(blocks_here, 3, own, BLK), ("gz", "gy"), split_axis=0, concat_axis=0, tiled=True
@@ -400,12 +467,12 @@
     )(branch_source, me, received)
     new_positions = new_blocks.transpose(2, 1, 0, 3).reshape(own, 3, walkers)
 
-    energies = jnp.concatenate(
-        [first[:, 0:1], energy_a[:, :split], energy_b[:, : geometries - 1 - split]], axis=1
-    )
-    log_sums = jnp.concatenate(
-        [first[:, 1:2], log_a[:, :split], log_b[:, : geometries - 1 - split]], axis=1
-    )
+    energies = jnp.concatenate([first[:, 0:1], energy_a, energy_b], axis=1)
+    log_sums = jnp.concatenate([first[:, 1:2], log_a, log_b], axis=1)
+    if early_rows is not None:
+        energies = jnp.concatenate([early_rows[0], energies], axis=0)
+        log_sums = jnp.concatenate([early_rows[1], log_sums], axis=0)
+        base = jnp.concatenate([early_rows[2], base], axis=0)
     nuclear = nuclear_repulsion(centers, charges)
     energies = (energies + base[:, 0:1] + nuclear[None, :, None]) * (1.0 / electrons)
     my_weights = lax.dynamic_slice_in_dim(weights.reshape(blocks_here, BLK), replica * mine, mine, 0)
@@ -416,19 +483,25 @@
     omega = alive_weights[:, None, :] * jnp.exp(2.0 * (log_sums - log_sums[:, 0:1]))
     sums = jnp.concatenate([jnp.sum(omega * energies, axis=(0, 2)), jnp.sum(omega, axis=(0, 2))])
     sums = jnp.pad(sums, (0, local_walkers - 2 * geometries)).reshape(mine, BLK)
-    rows = energies.transpose(1, 0, 2)
     replicas = lax.axis_size("gz")
-    for_group = rows.reshape(replicas, per_replica * mine, BLK)
-    for_all = jnp.concatenate([rows[0], alive_weights, sums, sums], axis=0)
-    group_rows, all_rows = pl.pallas_call(
-        exchange_kernel,
-        in_specs=[vmem, vmem],
-        out_specs=[vmem, vmem],
+    for_group = (
+        energies.reshape(mine, replicas, per_replica, BLK)
+        .transpose(1, 0, 2, 3)
+        .reshape(replicas, mine * per_replica, BLK)
+    )
+    for_all = jnp.concatenate([energies[:, 0], alive_weights, sums, sums], axis=0)
+    local_energy, estimate, new_weights = pl.pallas_call(
+        functools.partial(exchange_kernel, geometries, mine),
+        in_specs=[smem, vmem, vmem],
+        out_specs=[vmem, vmem, vmem],
         out_shape=[
-            jax.ShapeDtypeStruct((sources, per_replica * mine, BLK), jnp.float32),
-            jax.ShapeDtypeStruct((peers * sources, 4 * mine, BLK), jnp.float32),
+            jax.ShapeDtypeStruct((per_replica, walkers), jnp.float32),
+            jax.ShapeDtypeStruct((8, BLK), jnp.float32),
+            jax.ShapeDtypeStruct((blocks_here, BLK), jnp.float32),
         ],
         scratch_shapes=[
+            pltpu.VMEM((sources, per_replica * mine, BLK), jnp.float32),
+            pltpu.VMEM((peers * sources, 4 * mine, BLK), jnp.float32),
             pltpu.SemaphoreType.DMA((sources,)),
             pltpu.SemaphoreType.DMA((sources,)),
             pltpu.SemaphoreType.DMA((peers * sources,)),
@@ -436,23 +509,10 @@
         ],
         compiler_params=pltpu.CompilerParams(collective_id=0, has_side_effects=True),
         name="exchange",
-    )(for_group, for_all)
-    all_rows = all_rows.reshape(peers * sources, 4, mine, BLK)
-    total = jnp.sum(
-        all_rows[:, 2].reshape(peers * sources, local_walkers)[:, : 2 * geometries], axis=0
-    )
-    estimate = total[:geometries] / total[geometries:]
+    )(branch_source, for_group, for_all)
+    new_weights = new_weights.reshape(walkers)
     first_geometry = lax.axis_index("gz") * per_replica
-    local_energy = (
-        group_rows.reshape(sources, per_replica, local_walkers)
-        .transpose(1, 0, 2)
-        .reshape(per_replica, walkers)
-    )
-    kept = all_rows[:, 1] * jnp.exp(estimate[0] - all_rows[:, 0])
-    kept = kept.reshape(peers * blocks_here, BLK)
-    my_sources = lax.dynamic_slice_in_dim(branch_source, device * blocks_here, blocks_here, 0)
-    new_weights = jnp.take(kept, my_sources, axis=0).reshape(walkers)
-    my_estimate = lax.dynamic_slice_in_dim(estimate, first_geometry, per_replica, 0)
+    my_estimate = lax.dynamic_slice_in_dim(estimate[0], first_geometry, per_replica, 0)
     return (local_energy, my_estimate, new_positions, new_weights)
 
 

time: 142 us -> 137 us (0.965)
  waiting for transfers between devices: 21.6 us -> 9.93 us
  starting transfers between devices: 14.4 us -> 19.4 us
  local copies, waits for them, and re-layouts: 14.8 us -> 17.5 us
  other arithmetic: 3.97 us -> 2.16 us
    all_to_all x1 -> x2, waiting for transfers between devices: 18.8 us -> 6.97 us  [spread(): lax.all_to_all(x, ('gz', 'gy'), split_axis=0, concat_axis=0, tiled=True)]
    all_to_all x1 -> x2, starting transfers between devices: 6.49 us -> 10 us  [spread(): lax.all_to_all(x, ('gz', 'gy'), split_axis=0, concat_axis=0, tiled=True)]
    unnamed x31 -> x30, local copies, waits for them, and re-layouts: 4.61 us -> 7.15 us
    reshape x1 -> x0, local copies, waits for them, and re-layouts: 1.49 us -> none  [local(): group_rows.reshape(sources, per_replica, local_walkers).transpose(1, 0, 2)]
    all_to_all x1, starting transfers between devices: 3.55 us -> 5 us  [local(): lax.all_to_all(drift.reshape(blocks_here, 3, own, BLK), ('gz', 'gy'), spl...]
    pallas_call x4 -> x6, Pallas kernels: 77.3 us -> 78.7 us  [the longest x3 33.1 us: more(): pl.pallas_call(functools.partial(geometry_kernel, start, count, electrons...]
  transfers between devices with their start and end apart: 3 -> 4, of which waited for: 2 -> 2; matrix products, arithmetic and copies ran while one was open for 8% -> 6% of each run, Pallas kernels for 35% -> 42%
where the time goes in v2:
time: 137 us; the launch traced here: 136 us
  Pallas kernels  86.6 us (63%)
  starting transfers between devices  19.4 us (14%)
  local copies, waits for them, and re-layouts  17.5 us (13%)
  waiting for transfers between devices  9.93 us (7%)
  other arithmetic  2.16 us (2%)
    pallas_call x3, Pallas kernels, more(): pl.pallas_call(functools.partial(geometry_kernel, start, count, electrons...  33.1 us
    pallas_call x2, Pallas kernels, pairs(): pl.pallas_call(functools.partial(pair_kernel, own, sources), grid=(blocks...  27.9 us
    pallas_call x1, Pallas kernels, local(): pl.pallas_call(functools.partial(exchange_kernel, geometries, mine), in_s...  17.7 us
    all_to_all x2, starting transfers between devices, spread(): lax.all_to_all(x, ('gz', 'gy'), split_axis=0, concat_axis=0, tiled=True)  10 us
    unnamed x30, local copies, waits for them, and re-layouts  7.15 us
    all_to_all x2, waiting for transfers between devices, spread(): lax.all_to_all(x, ('gz', 'gy'), split_axis=0, concat_axis=0, tiled=True)  6.97 us
    pallas_call x1, Pallas kernels, local(): pl.pallas_call(functools.partial(pack_kernel, blocks_here, capacity), in_...  5.03 us
    all_to_all x1, starting transfers between devices, local(): lax.all_to_all(drift.reshape(blocks_here, 3, own, BLK), ('gz', 'gy'), spl...  5 us
  transfers between devices with their start and end apart: 4, of which 2 were waited for; matrix products, arithmetic and copies ran while one was open for 6% of the time, Pallas kernels for 42%

profile of v2, /device:TPU:0, one launch (start us, length us, event | category | flops | bytes accessed | tf_op | source)
XLA Modules:
  0.0 136.5 jit_solution(16192726418235298224)
XLA Ops:
  0.6 1.1 copy-done
  1.8 1.0 fusion.8
  2.8 0.7 slice.84
  3.4 6.5 %all-to-all-start.1 = ((f32[8,1,3,16,128]{4,3,2,1,0:T(8,128)}), f32[8,1,3,16,128]{4,3,2,1,0:T(8,128)S(1)}, u32[]{:S(2)}, u32[]{:S(2)}) async-start(f32[8,1,3,16,128]{4,3,2,1,0:T(8,128)} %slice.84), calls=%async_computation.1 | async-start | bytes 393216 | tf_op jit(solution)/shard_map/all_to_all | solution.py:346
  9.9 0.9 slice.80
  10.9 7.0 %all-to-all-done.1.pos = f32[8,1,3,16,128]{4,3,2,1,0:T(8,128)S(1)} async-done(((f32[8,1,3,16,128]{4,3,2,1,0:T(8,128)}), f32[8,1,3,16,128]{4,3,2,1,0:T(8,128)S(1)}, u32[]{:S(2)}, u32[]{:S(2)}) %all-to-all-start.1) | async-done | bytes 196640 | tf_op jit(solution)/shard_map/all_to_all | solution.py:346
  17.8 3.5 %all-to-all-start = ((f32[8,3,3,16,128]{4,3,2,1,0:T(8,128)}), f32[8,3,3,16,128]{4,3,2,1,0:T(8,128)S(1)}, u32[]{:S(2)}, u32[]{:S(2)}) async-start(f32[8,3,3,16,128]{4,3,2,1,0:T(8,128)} %slice.80), calls=%async_computation | async-start | bytes 1179648 | tf_op jit(solution)/shard_map/all_to_all | solution.py:346
  23.1 6.9 %pairs_0.1 = (f32[8,4,3,16,128]{4,3,2,1,0:T(8,128)S(1)}, f32[1,6,128,128]{3,2,1,0:T(8,128)S(1)}, f32[1,8,128]{2,1,0:T(8,128)S(1)}, f32[1,8,128]{2,1,0:T(8,128)S(1)}) custom-call(f32[8,16,16,128]{3,2,1,0:T(8,128)S(1)} %broadcast_in_dim.2.consts, f32[8,1,3,16,128]{4,3,2,1,0:T(8,128)S(1)} %all-to-all-done.1.pos), custom_call_target="tpu_custom_call" | custom-call | flops 25000000 | bytes 1000000 | tf_op jit(solution)/shard_map/pairs_0/pallas_call | solution.py:378
  30.0 0.9 copy-done.1
  30.9 8.2 %geometries_1_1.1 = (f32[1,8,128]{2,1,0:T(8,128)S(1)}, f32[1,8,128]{2,1,0:T(8,128)S(1)}) custom-call(f32[8,16,16,128]{3,2,1,0:T(8,128)S(1)} %broadcast_in_dim.2.consts, f32[1,6,128,128]{3,2,1,0:T(8,128)S(1)} %get-tuple-element.28.jgrad), custom_call_target="tpu_custom_call" | custom-call | flops 52500000 | bytes 2000000 | tf_op jit(solution)/shard_map/geometries_1_1/pallas_call | solution.py:410
  39.2 0.8 copy-done.4
  40.1 1.1 copy-done.2
  41.2 1.1 copy-done.5
  42.3 20.9 %pairs_1.1 = (f32[8,4,3,16,128]{4,3,2,1,0:T(8,128)S(1)}, f32[3,6,128,128]{3,2,1,0:T(8,128)S(1)}, f32[3,8,128]{2,1,0:T(8,128)S(1)}, f32[3,8,128]{2,1,0:T(8,128)S(1)}) custom-call(f32[8,16,16,128]{3,2,1,0:T(8,128)S(1)} %broadcast_in_dim.2.consts, f32[8,3,3,16,128]{4,3,2,1,0:T(8,128)S(1)} %copy-done.5, ...), custom_call_target="tpu_custom_call", output_to_operand_aliasing={{0}: (2, {})} | custom-call | flops 75000000 | bytes 3000000 | tf_op jit(solution)/shard_map/pairs_1/pallas_call | solution.py:378
  63.2 0.9 copy-done.3
  64.1 5.0 %all-to-all-start.2 = ((f32[32,3,16,128]{3,2,1,0:T(8,128)}), f32[32,3,16,128]{3,2,1,0:T(8,128)}, u32[]{:S(2)}, u32[]{:S(2)}) async-start(f32[32,3,16,128]{3,2,1,0:T(8,128)} %bitcast.49), calls=%async_computation.2 | async-start | bytes 1572864 | tf_op jit(solution)/shard_map/all_to_all | solution.py:442
  69.5 0.8 dynamic-slice_select_fusion
  70.2 2.1 %bitcast_bitcast_fusion.noise = f32[32,3,16,128]{3,2,1,0:T(8,128)} fusion(f32[16,3,4096]{2,0,1:T(8,128)} %param.11), kind=kLoop, calls=%fused_computation.1 | loop fusion | bytes 1572864 | tf_op jit(solution)/shard_map/transpose | solution.py:338
  72.4 14.2 %geometries_1_3.1 = (f32[3,8,128]{2,1,0:T(8,128)S(1)}, f32[3,8,128]{2,1,0:T(8,128)S(1)}) custom-call(f32[8,16,16,128]{3,2,1,0:T(8,128)S(1)} %broadcast_in_dim.2.consts, f32[3,6,128,128]{3,2,1,0:T(8,128)S(1)} %get-tuple-element.39.jgrad), custom_call_target="tpu_custom_call" | custom-call | flops 90000000 | bytes 6000000 | tf_op jit(solution)/shard_map/geometries_1_3/pallas_call | solution.py:410
  86.6 3.0 %all-to-all-done.2.drift = f32[32,3,16,128]{3,2,1,0:T(8,128)} async-done(((f32[32,3,16,128]{3,2,1,0:T(8,128)}), f32[32,3,16,128]{3,2,1,0:T(8,128)}, u32[]{:S(2)}, u32[]{:S(2)}) %all-to-all-start.2) | async-done | bytes 786464 | tf_op jit(solution)/shard_map/all_to_all | solution.py:442
  89.6 5.0 %pack.1 = f32[64,3,16,128]{3,2,1,0:T(8,128)} custom-call(s32[128]{0:T(128)} %source_ref.5, s32[1]{0:T(128)} %bitcast.7.me_ref, f32[32,3,16,128]{3,2,1,0:T(8,128)} %get-tuple-element.55.pos, f32[32,3,16,128]{3,2,1,0:T(8,128)} %all-to-all-done.2.drift, f32[32,3,16,128]{3,2,1,0:T(8,128)} %bitcast_bitcast_fusion.noise), custom_call_target="tpu_custom_call" | custom-call | tf_op jit(solution)/shard_map/pack/pallas_call | solution.py:449
  94.6 4.3 %all-to-all-start.3 = ((f32[64,3,16,128]{3,2,1,0:T(8,128)}), f32[64,3,16,128]{3,2,1,0:T(8,128)}, u32[]{:S(2)}, u32[]{:S(2)}) async-start(f32[64,3,16,128]{3,2,1,0:T(8,128)} %pack.1), calls=%async_computation.3 | async-start | bytes 3145728 | tf_op jit(solution)/shard_map/all_to_all | solution.py:459
  99.0 10.7 %geometries_5_3.1 = (f32[3,8,128]{2,1,0:T(8,128)S(1)}, f32[3,8,128]{2,1,0:T(8,128)S(1)}) custom-call(f32[8,16,16,128]{3,2,1,0:T(8,128)S(1)} %broadcast_in_dim.2.consts, f32[3,6,128,128]{3,2,1,0:T(8,128)S(1)} %get-tuple-element.39.jgrad), custom_call_target="tpu_custom_call" | custom-call | flops 67500000 | bytes 6000000 | tf_op jit(solution)/shard_map/geometries_5_3/pallas_call | solution.py:410
  109.7 0.6 copy.73
  110.7 0.6 pad_maximum_fusion.1.all_in
  111.3 17.7 %exchange.1 = (f32[4,4096]{1,0:T(4,128)}, f32[8,128]{1,0:T(8,128)}, f32[32,128]{1,0:T(8,128)}) custom-call(s32[128]{0:T(128)} %source_ref.5, f32[2,16,128]{2,1,0:T(8,128)} %bitcast.55, f32[16,128]{1,0:T(8,128)} %pad_maximum_fusion.1.all_in), custom_call_target="tpu_custom_call" | custom-call | tf_op jit(solution)/shard_map/exchange/pallas_call | solution.py:493
  129.0 0.7 slice.79
  129.7 0.6 dynamic-slice_bitcast_fusion
  130.3 2.9 %unpack.1 = f32[32,3,16,128]{3,2,1,0:T(8,128)} custom-call(s32[128]{0:T(128)} %source_ref.5, s32[1]{0:T(128)} %bitcast.7.me_ref, f32[64,3,16,128]{3,2,1,0:T(8,128)} %all-to-all-done.3.received), custom_call_target="tpu_custom_call" | custom-call | tf_op jit(solution)/shard_map/unpack/pallas_call | solution.py:460
  133.2 2.1 %copy_bitcast_fusion = f32[16,3,4096]{2,0,1:T(8,128)} fusion(f32[32,3,16,128]{3,2,1,0:T(8,128)} %unpack.1), kind=kLoop, calls=%fused_computation | loop fusion | bytes 1572864 | tf_op jit(solution)/shard_map/reshape | solution.py:468
  135.3 0.6 copy.89
  135.9 0.6 copy.90
  (73 shorter events, 2.6 us)
Async XLA Ops:
  0.6 1.1 copy-start
  2.8 8.1 %copy-start.8 = (f32[8,16,3]{1,0,2:T(8,128)S(1)}, f32[8,16,3]{1,0,2:T(8,128)}, u32[]{:S(2)}) copy-start(f32[8,16,3]{1,0,2:T(8,128)} %param.13) | copy-start | bytes 4612
  2.8 8.1 %copy-start.10 = (f32[16,3]{0,1:T(4,128)S(1)}, f32[16,3]{0,1:T(4,128)}, u32[]{:S(2)}) copy-start(f32[16,3]{0,1:T(4,128)} %param.12) | copy-start | bytes 580
  3.4 18.1 %copy-start.9 = (f32[16]{0:T(128)S(1)}, f32[16]{0:T(128)}, u32[]{:S(2)}) copy-start(f32[16]{0:T(128)} %param.14) | copy-start | bytes 196
  3.4 18.6 %copy-start.12 = (f32[16]{0:T(128)S(1)}, f32[16]{0:T(128)}, u32[]{:S(2)}) copy-start(f32[16]{0:T(128)} %param.16) | copy-start | bytes 196
  3.4 18.6 %copy-start.11 = (f32[16]{0:T(128)S(1)}, f32[16]{0:T(128)}, u32[]{:S(2)}) copy-start(f32[16]{0:T(128)} %param.15) | copy-start | bytes 196
  3.4 14.4 %all-to-all-start.1 = ((f32[8,1,3,16,128]{4,3,2,1,0:T(8,128)}), f32[8,1,3,16,128]{4,3,2,1,0:T(8,128)S(1)}, u32[]{:S(2)}, u32[]{:S(2)}) async-start(f32[8,1,3,16,128]{4,3,2,1,0:T(8,128)} %slice.84), calls=%async_computation.1 | async-start | bytes 393216 | tf_op jit(solution)/shard_map/all_to_all | solution.py:346
  17.8 21.4 %all-to-all-start = ((f32[8,3,3,16,128]{4,3,2,1,0:T(8,128)}), f32[8,3,3,16,128]{4,3,2,1,0:T(8,128)S(1)}, u32[]{:S(2)}, u32[]{:S(2)}) async-start(f32[8,3,3,16,128]{4,3,2,1,0:T(8,128)} %slice.80), calls=%async_computation | async-start | bytes 1179648 | tf_op jit(solution)/shard_map/all_to_all | solution.py:346
  30.0 0.9 copy-start.1
  39.2 0.8 copy-start.4
  40.1 1.1 copy-start.2
  41.2 1.1 copy-start.5
  42.3 27.1 %copy-start.13 = (s32[32]{0:T(128)S(1)}, s32[32]{0:T(128)}, u32[]{:S(2)}) copy-start(s32[32]{0:T(128)} %param.18) | copy-start | bytes 388
  63.2 0.9 copy-start.3
  64.1 25.5 %all-to-all-start.2 = ((f32[32,3,16,128]{3,2,1,0:T(8,128)}), f32[32,3,16,128]{3,2,1,0:T(8,128)}, u32[]{:S(2)}, u32[]{:S(2)}) async-start(f32[32,3,16,128]{3,2,1,0:T(8,128)} %bitcast.49), calls=%async_computation.2 | async-start | bytes 1572864 | tf_op jit(solution)/shard_map/all_to_all | solution.py:442
  94.6 35.7 %all-to-all-start.3 = ((f32[64,3,16,128]{3,2,1,0:T(8,128)}), f32[64,3,16,128]{3,2,1,0:T(8,128)}, u32[]{:S(2)}, u32[]{:S(2)}) async-start(f32[64,3,16,128]{3,2,1,0:T(8,128)} %pack.1), calls=%async_computation.3 | async-start | bytes 3145728 | tf_op jit(solution)/shard_map/all_to_all | solution.py:459
  130.3 5.0 %copy-start.6 = (f32[4,4096]{1,0:T(4,128)S(1)}, f32[4,4096]{1,0:T(4,128)}, u32[]{:S(2)}) copy-start(f32[4,4096]{1,0:T(4,128)} %get-tuple-element.70) | copy-start | bytes 196612
  130.3 5.6 %copy-start.7 = (f32[32,128]{1,0:T(8,128)S(1)}, f32[32,128]{1,0:T(8,128)}, u32[]{:S(2)}) copy-start(f32[32,128]{1,0:T(8,128)} %get-tuple-element.49) | copy-start | bytes 49156

commit v3 on v2

--- a/solution.py
+++ b/solution.py
@@ -397,7 +397,7 @@
                 pltpu.VMEM((3, electrons, BLK), jnp.float32),
             ],
             input_output_aliases={2: 0} if previous else {},
-            compiler_params=pltpu.CompilerParams(vmem_limit_bytes=32 * 2**20),
+            compiler_params=pltpu.CompilerParams(vmem_limit_bytes=60 * 2**20),
             cost_estimate=pl.CostEstimate(
                 flops=blocks * 25_000_000, bytes_accessed=blocks * 1_000_000, transcendentals=0
             ),
@@ -413,7 +413,7 @@
             in_specs=[table_spec, grad_spec],
             out_specs=[lane_spec, lane_spec],
             out_shape=[lane_shape, lane_shape],
-            compiler_params=pltpu.CompilerParams(vmem_limit_bytes=16 * 2**20),
+            compiler_params=pltpu.CompilerParams(vmem_limit_bytes=60 * 2**20),
             cost_estimate=pl.CostEstimate(
                 flops=blocks * count * 7_500_000,
                 bytes_accessed=blocks * 2_000_000,

time: 137 us -> 148 us (1.080)
  Pallas kernels: 86.6 us -> 97.5 us
  local copies, waits for them, and re-layouts: 17.5 us -> 20.3 us
  waiting for transfers between devices: 9.93 us -> 7.6 us
    pallas_call x3, Pallas kernels: 33.1 us -> 38.9 us  [more(): pl.pallas_call(functools.partial(geometry_kernel, start, count, electrons...]
    pallas_call x2, Pallas kernels: 27.9 us -> 32.2 us  [pairs(): pl.pallas_call(functools.partial(pair_kernel, own, sources), grid=(blocks...]
    pallas_call x4, local copies, waits for them, and re-layouts: 0.02 us -> 2.84 us  [more(): pl.pallas_call(functools.partial(geometry_kernel, start, count, electrons...]
    all_to_all x1, waiting for transfers between devices: 2.96 us -> 0.64 us  [local(): lax.all_to_all(drift.reshape(blocks_here, 3, own, BLK), ('gz', 'gy'), spl...]
    unnamed x30 -> x36, local copies, waits for them, and re-layouts: 7.15 us -> 5.32 us
  transfers between devices with their start and end apart: 4 -> 4, of which waited for: 2 -> 2; matrix products, arithmetic and copies ran while one was open for 6% -> 9% of each run, Pallas kernels for 42% -> 45%
where the time goes in v3:
time: 148 us; the launch traced here: 147 us
  Pallas kernels  97.5 us (66%)
  local copies, waits for them, and re-layouts  20.3 us (14%)
  starting transfers between devices  18.7 us (13%)
  waiting for transfers between devices  7.6 us (5%)
  other arithmetic  2.16 us (1%)
    pallas_call x3, Pallas kernels, more(): pl.pallas_call(functools.partial(geometry_kernel, start, count, electrons...  38.9 us
    pallas_call x2, Pallas kernels, pairs(): pl.pallas_call(functools.partial(pair_kernel, own, sources), grid=(blocks...  32.2 us
    pallas_call x1, Pallas kernels, local(): pl.pallas_call(functools.partial(exchange_kernel, geometries, mine), in_s...  18.6 us
    all_to_all x2, starting transfers between devices, spread(): lax.all_to_all(x, ('gz', 'gy'), split_axis=0, concat_axis=0, tiled=True)  10 us
    all_to_all x2, waiting for transfers between devices, spread(): lax.all_to_all(x, ('gz', 'gy'), split_axis=0, concat_axis=0, tiled=True)  6.95 us
    unnamed x36, local copies, waits for them, and re-layouts  5.32 us
    pallas_call x1, Pallas kernels, local(): pl.pallas_call(functools.partial(pack_kernel, blocks_here, capacity), in_...  5.05 us
    all_to_all x1, starting transfers between devices, local(): lax.all_to_all(drift.reshape(blocks_here, 3, own, BLK), ('gz', 'gy'), spl...  5.01 us
  transfers between devices with their start and end apart: 4, of which 2 were waited for; matrix products, arithmetic and copies ran while one was open for 9% of the time, Pallas kernels for 45%

profile of v3, /device:TPU:0, one launch (start us, length us, event | category | flops | bytes accessed | tf_op | source)
XLA Modules:
  0.0 147.2 jit_solution(10014264274677640793)
XLA Ops:
  0.6 1.1 copy-done
  1.8 1.0 fusion.8
  2.8 0.7 slice.84
  3.4 6.5 %all-to-all-start.1 = ((f32[8,1,3,16,128]{4,3,2,1,0:T(8,128)}), f32[8,1,3,16,128]{4,3,2,1,0:T(8,128)S(1)}, u32[]{:S(2)}, u32[]{:S(2)}) async-start(f32[8,1,3,16,128]{4,3,2,1,0:T(8,128)} %slice.84), calls=%async_computation.1 | async-start | bytes 393216 | tf_op jit(solution)/shard_map/all_to_all | solution.py:346
  9.9 0.9 slice.80
  10.9 7.0 %all-to-all-done.1.pos = f32[8,1,3,16,128]{4,3,2,1,0:T(8,128)S(1)} async-done(((f32[8,1,3,16,128]{4,3,2,1,0:T(8,128)}), f32[8,1,3,16,128]{4,3,2,1,0:T(8,128)S(1)}, u32[]{:S(2)}, u32[]{:S(2)}) %all-to-all-start.1) | async-done | bytes 196640 | tf_op jit(solution)/shard_map/all_to_all | solution.py:346
  17.8 3.5 %all-to-all-start = ((f32[8,3,3,16,128]{4,3,2,1,0:T(8,128)}), f32[8,3,3,16,128]{4,3,2,1,0:T(8,128)S(1)}, u32[]{:S(2)}, u32[]{:S(2)}) async-start(f32[8,3,3,16,128]{4,3,2,1,0:T(8,128)} %slice.80), calls=%async_computation | async-start | bytes 1179648 | tf_op jit(solution)/shard_map/all_to_all | solution.py:346
  22.8 1.3 broadcast_in_dim.2.consts
  24.1 9.0 %pairs_0.1 = (f32[8,4,3,16,128]{4,3,2,1,0:T(8,128)}, f32[1,6,128,128]{3,2,1,0:T(8,128)}, f32[1,8,128]{2,1,0:T(8,128)}, f32[1,8,128]{2,1,0:T(8,128)}) custom-call(f32[8,16,16,128]{3,2,1,0:T(8,128)} %broadcast_in_dim.2.consts, f32[8,1,3,16,128]{4,3,2,1,0:T(8,128)} %copy-done.4), custom_call_target="tpu_custom_call" | custom-call | flops 25000000 | bytes 1000000 | tf_op jit(solution)/shard_map/pairs_0/pallas_call | solution.py:378
  33.1 10.1 %geometries_1_1.1 = (f32[1,8,128]{2,1,0:T(8,128)}, f32[1,8,128]{2,1,0:T(8,128)}) custom-call(f32[8,16,16,128]{3,2,1,0:T(8,128)} %broadcast_in_dim.2.consts, f32[1,6,128,128]{3,2,1,0:T(8,128)} %get-tuple-element.28.jgrad), custom_call_target="tpu_custom_call" | custom-call | flops 52500000 | bytes 2000000 | tf_op jit(solution)/shard_map/geometries_1_1/pallas_call | solution.py:410
  43.2 0.7 copy.63
  43.9 0.7 copy.65
  44.6 0.7 fusion.11
  45.3 0.8 copy-done.3
  46.1 23.2 %pairs_1.1 = (f32[8,4,3,16,128]{4,3,2,1,0:T(8,128)}, f32[3,6,128,128]{3,2,1,0:T(8,128)}, f32[3,8,128]{2,1,0:T(8,128)}, f32[3,8,128]{2,1,0:T(8,128)}) custom-call(f32[8,16,16,128]{3,2,1,0:T(8,128)} %broadcast_in_dim.2.consts, f32[8,3,3,16,128]{4,3,2,1,0:T(8,128)} %copy-done.3, ...), custom_call_target="tpu_custom_call", output_to_operand_aliasing={{0}: (2, {})} | custom-call | flops 75000000 | bytes 3000000 | tf_op jit(solution)/shard_map/pairs_1/pallas_call | solution.py:378
  69.3 5.0 %all-to-all-start.2 = ((f32[32,3,16,128]{3,2,1,0:T(8,128)}), f32[32,3,16,128]{3,2,1,0:T(8,128)S(1)}, u32[]{:S(2)}, u32[]{:S(2)}) async-start(f32[32,3,16,128]{3,2,1,0:T(8,128)} %bitcast.49), calls=%async_computation.2 | async-start | bytes 1572864 | tf_op jit(solution)/shard_map/all_to_all | solution.py:442
  74.7 0.8 dynamic-slice_select_fusion
  75.5 0.9 bitcast_bitcast_fusion.noise
  76.4 16.1 %geometries_1_3.1 = (f32[3,8,128]{2,1,0:T(8,128)}, f32[3,8,128]{2,1,0:T(8,128)}) custom-call(f32[8,16,16,128]{3,2,1,0:T(8,128)} %broadcast_in_dim.2.consts, f32[3,6,128,128]{3,2,1,0:T(8,128)} %get-tuple-element.39.jgrad), custom_call_target="tpu_custom_call" | custom-call | flops 90000000 | bytes 6000000 | tf_op jit(solution)/shard_map/geometries_1_3/pallas_call | solution.py:410
  92.6 0.7 copy.67
  93.3 0.7 copy.75
  94.7 0.9 copy-done.2
  95.6 5.0 %pack.1 = f32[64,3,16,128]{3,2,1,0:T(8,128)} custom-call(s32[128]{0:T(128)} %source_ref.5, s32[1]{0:T(128)} %bitcast.7.me_ref, f32[32,3,16,128]{3,2,1,0:T(8,128)} %get-tuple-element.55.pos, f32[32,3,16,128]{3,2,1,0:T(8,128)} %copy-done.2, f32[32,3,16,128]{3,2,1,0:T(8,128)} %bitcast_bitcast_fusion.noise), custom_call_target="tpu_custom_call" | custom-call | tf_op jit(solution)/shard_map/pack/pallas_call | solution.py:449
  100.6 3.7 %all-to-all-start.3 = ((f32[64,3,16,128]{3,2,1,0:T(8,128)}), f32[64,3,16,128]{3,2,1,0:T(8,128)S(1)}, u32[]{:S(2)}, u32[]{:S(2)}) async-start(f32[64,3,16,128]{3,2,1,0:T(8,128)} %pack.1), calls=%async_computation.3 | async-start | bytes 3145728 | tf_op jit(solution)/shard_map/all_to_all | solution.py:459
  104.4 12.6 %geometries_5_3.1 = (f32[3,8,128]{2,1,0:T(8,128)}, f32[3,8,128]{2,1,0:T(8,128)}) custom-call(f32[8,16,16,128]{3,2,1,0:T(8,128)} %broadcast_in_dim.2.consts, f32[3,6,128,128]{3,2,1,0:T(8,128)} %get-tuple-element.39.jgrad), custom_call_target="tpu_custom_call" | custom-call | flops 67500000 | bytes 6000000 | tf_op jit(solution)/shard_map/geometries_5_3/pallas_call | solution.py:410
  117.0 0.7 copy.69
  118.4 0.7 copy.76
  120.0 18.6 %exchange.1 = (f32[4,4096]{1,0:T(4,128)}, f32[8,128]{1,0:T(8,128)}, f32[32,128]{1,0:T(8,128)}) custom-call(s32[128]{0:T(128)} %source_ref.5, f32[2,16,128]{2,1,0:T(8,128)} %bitcast.52, f32[16,128]{1,0:T(8,128)} %pad_maximum_fusion.1.all_in), custom_call_target="tpu_custom_call" | custom-call | tf_op jit(solution)/shard_map/exchange/pallas_call | solution.py:493
  138.6 0.7 slice.79
  139.9 1.2 copy-done.1
  141.0 2.9 %unpack.1 = f32[32,3,16,128]{3,2,1,0:T(8,128)} custom-call(s32[128]{0:T(128)} %source_ref.5, s32[1]{0:T(128)} %bitcast.7.me_ref, f32[64,3,16,128]{3,2,1,0:T(8,128)} %copy-done.1), custom_call_target="tpu_custom_call" | custom-call | tf_op jit(solution)/shard_map/unpack/pallas_call | solution.py:460
  143.9 2.1 %copy_bitcast_fusion = f32[16,3,4096]{2,0,1:T(8,128)} fusion(f32[32,3,16,128]{3,2,1,0:T(8,128)} %unpack.1), kind=kLoop, calls=%fused_computation | loop fusion | bytes 1572864 | tf_op jit(solution)/shard_map/reshape | solution.py:468
  (79 shorter events, 5.9 us)
Async XLA Ops:
  0.6 1.1 copy-start
  2.8 8.1 %copy-start.10 = (f32[8,16,3]{1,0,2:T(8,128)S(1)}, f32[8,16,3]{1,0,2:T(8,128)}, u32[]{:S(2)}) copy-start(f32[8,16,3]{1,0,2:T(8,128)} %param.13) | copy-start | bytes 4612
  2.8 8.1 %copy-start.13 = (f32[16,3]{0,1:T(4,128)S(1)}, f32[16,3]{0,1:T(4,128)}, u32[]{:S(2)}) copy-start(f32[16,3]{0,1:T(4,128)} %param.12) | copy-start | bytes 580
  3.4 18.1 %copy-start.12 = (f32[16]{0:T(128)S(1)}, f32[16]{0:T(128)}, u32[]{:S(2)}) copy-start(f32[16]{0:T(128)} %param.14) | copy-start | bytes 196
  3.4 18.6 %copy-start.15 = (f32[16]{0:T(128)S(1)}, f32[16]{0:T(128)}, u32[]{:S(2)}) copy-start(f32[16]{0:T(128)} %param.16) | copy-start | bytes 196
  3.4 18.6 %copy-start.14 = (f32[16]{0:T(128)S(1)}, f32[16]{0:T(128)}, u32[]{:S(2)}) copy-start(f32[16]{0:T(128)} %param.15) | copy-start | bytes 196
  3.4 14.4 %all-to-all-start.1 = ((f32[8,1,3,16,128]{4,3,2,1,0:T(8,128)}), f32[8,1,3,16,128]{4,3,2,1,0:T(8,128)S(1)}, u32[]{:S(2)}, u32[]{:S(2)}) async-start(f32[8,1,3,16,128]{4,3,2,1,0:T(8,128)} %slice.84), calls=%async_computation.1 | async-start | bytes 393216 | tf_op jit(solution)/shard_map/all_to_all | solution.py:346
  17.8 6.3 %copy-start.4 = (f32[8,1,3,16,128]{4,3,2,1,0:T(8,128)}, f32[8,1,3,16,128]{4,3,2,1,0:T(8,128)S(1)}, u32[]{:S(2)}) copy-start(f32[8,1,3,16,128]{4,3,2,1,0:T(8,128)S(1)} %all-to-all-done.1.pos) | copy-start | bytes 589828
  17.8 27.5 %all-to-all-start = ((f32[8,3,3,16,128]{4,3,2,1,0:T(8,128)}), f32[8,3,3,16,128]{4,3,2,1,0:T(8,128)S(1)}, u32[]{:S(2)}, u32[]{:S(2)}) async-start(f32[8,3,3,16,128]{4,3,2,1,0:T(8,128)} %slice.80), calls=%async_computation | async-start | bytes 1179648 | tf_op jit(solution)/shard_map/all_to_all | solution.py:346
  45.3 0.8 copy-start.3
  46.1 28.5 %copy-start.16 = (s32[32]{0:T(128)S(1)}, s32[32]{0:T(128)}, u32[]{:S(2)}) copy-start(s32[32]{0:T(128)} %param.18) | copy-start | bytes 388
  46.1 29.3 %copy-start.5 = (f32[16,3,4096]{2,0,1:T(8,128)S(1)}, f32[16,3,4096]{2,0,1:T(8,128)}, u32[]{:S(2)}) copy-start(f32[16,3,4096]{2,0,1:T(8,128)} %param.11) | copy-start | bytes 2359300
  69.3 7.1 %copy-start.8 = (f32[3,8,128]{2,1,0:T(8,128)S(1)}, f32[3,8,128]{2,1,0:T(8,128)}, u32[]{:S(2)}) copy-start(f32[3,8,128]{2,1,0:T(8,128)} %get-tuple-element.35) | copy-start | bytes 36868
  69.3 25.4 %all-to-all-start.2 = ((f32[32,3,16,128]{3,2,1,0:T(8,128)}), f32[32,3,16,128]{3,2,1,0:T(8,128)S(1)}, u32[]{:S(2)}, u32[]{:S(2)}) async-start(f32[32,3,16,128]{3,2,1,0:T(8,128)} %bitcast.49), calls=%async_computation.2 | async-start | bytes 1572864 | tf_op jit(solution)/shard_map/all_to_all | solution.py:442
  75.5 18.5 %copy-start.9 = (f32[3,8,128]{2,1,0:T(8,128)S(1)}, f32[3,8,128]{2,1,0:T(8,128)}, u32[]{:S(2)}) copy-start(f32[3,8,128]{2,1,0:T(8,128)} %get-tuple-element.42) | copy-start | bytes 36868
  75.5 18.5 %copy-start.11 = (f32[1,8,128]{2,1,0:T(8,128)S(1)}, f32[1,8,128]{2,1,0:T(8,128)}, u32[]{:S(2)}) copy-start(f32[1,8,128]{2,1,0:T(8,128)} %get-tuple-element.41) | copy-start | bytes 12292
  94.7 0.9 copy-start.2
  100.6 39.2 %all-to-all-start.3 = ((f32[64,3,16,128]{3,2,1,0:T(8,128)}), f32[64,3,16,128]{3,2,1,0:T(8,128)S(1)}, u32[]{:S(2)}, u32[]{:S(2)}) async-start(f32[64,3,16,128]{3,2,1,0:T(8,128)} %pack.1), calls=%async_computation.3 | async-start | bytes 3145728 | tf_op jit(solution)/shard_map/all_to_all | solution.py:459
  139.9 6.1 %copy-start.6 = (f32[4,4096]{1,0:T(4,128)S(1)}, f32[4,4096]{1,0:T(4,128)}, u32[]{:S(2)}) copy-start(f32[4,4096]{1,0:T(4,128)} %get-tuple-element.70) | copy-start | bytes 196612
  139.9 6.7 %copy-start.7 = (f32[32,128]{1,0:T(8,128)S(1)}, f32[32,128]{1,0:T(8,128)}, u32[]{:S(2)}) copy-start(f32[32,128]{1,0:T(8,128)} %get-tuple-element.49) | copy-start | bytes 49156
  139.9 1.2 copy-start.1
